TPU v7x, 32 devices: a whole 2x2x4 slice. The times are simulated.
32 devices in a mesh: gx: 8 (over z, core), gy: 4 (over y, x).
Axes of the slice: x: 2, y: 2, z: 4, core: 2. Of those that a mesh axis runs over, the one named last changes fastest.
Arguments:
- residual: float32 [3, 128, 64, 128], P(None, 'gx', 'gy'), may hold values from -6 to 6
- stiffness: float32 [128, 64], P('gx', 'gy'), may hold values from 0.5 to 2
- local_inverse: bfloat16 [8, 4, 1024, 1024], P('gx', 'gy'), as said below
- coarse_basis: bfloat16 [8, 4, 8, 1024], P('gx', 'gy'), may hold values from -0.5 to 0.5
- coarse_rows: bfloat16 [8, 4, 8, 256], P('gx', 'gy'), as said below
- send_rows: int32 [8, 4, 4, 64], P('gx', 'gy'), may hold values from 0 to 767, as said below
- partition_map: int32 [32], replicated, may hold values from 0 to 31, as said below
Outputs:
- solution: float32 [3, 128, 64, 128], P(None, 'gx', 'gy')
- final: float32 [3, 128, 64, 128], P(None, 'gx', 'gy')
Inputs may be any that keep to these rules, and one draw needn't show every extreme that they name: `send_rows`: for each subdomain, the lists j = 0, 1 (lower and upper neighbour along gx) and j = 2, 3 (lower and upper neighbour along gy) each name 64 distinct owned rows, all of them in the two layers of cells nearest that neighbour. `partition_map`: A permutation of the device numbers. `coarse_rows`: with its columns put in device order through partition_map, the 256-square matrix S is symmetric. `local_inverse`: each subdomain's block is symmetric.
All inputs are finite; a program needn't handle non-finite values.
Results may differ from a plain program's by a relative error of at most 0.0057.
Values may be sent and summed in bfloat16 or wider, within the bound.
A program may use at most 64 MiB of HBM per device.

v0:
```python
import functools

import jax
import jax.numpy as jnp
from jax import lax
from jax.experimental import pallas as pl
from jax.experimental.pallas import tpu as pltpu
from jax.sharding import PartitionSpec as P

MESH = pl.DeviceIdType.MESH
F32 = jnp.float32
BF16 = jnp.bfloat16
HIGH = lax.Precision.HIGHEST


def dot(x, y, **kw):
    return jnp.dot(x, y, preferred_element_type=F32, **kw)


def tdot(x, y):
    return lax.dot_general(x, y, (((0,), (0,)), ((), ())), preferred_element_type=F32)


def fiota(shape, axis):
    return lax.broadcasted_iota(jnp.int32, shape, axis).astype(F32)


def fdiv(x, n):
    return jnp.floor((x + 0.5) * (1.0 / n))


def kernel(
    gx, gy, dims,
    res_hbm, stiff_hbm, inv_hbm, basis_hbm, crows_hbm, lists_hbm, pmap_hbm,
    sol_ref, fin_ref,
    res_v, stiff_ref, inv_v, basis_ref, crows_ref, lists_ref, pmap_ref, sub, sel, selt, outs, backs, backr, hs, hr, allbuf,
    sext, bsend, brecv, bextf, cmat, acmat, csend, diag, m_lo, m_hi, xs, mid,
    lsem, nsem_s, nsem_r, csem_s, csem_r, g1s, g1r, g2s, g2r,
):
    comps, cx, cy, nv = dims
    halo = hr.shape[2]
    hrows = (comps * cy, comps * cy, comps * cx, comps * cx)
    own = comps * cx * cy
    layer = cx * cy
    ov = lists_ref.shape[1]
    kw, kd = crows_ref.shape
    a = lax.axis_index("gx")
    b = lax.axis_index("gy")

    wanted = [
        (lists_hbm, lists_ref), (res_hbm, res_v), (pmap_hbm, pmap_ref), (crows_hbm, crows_ref),
        (basis_hbm, basis_ref), (stiff_hbm, stiff_ref), (inv_hbm, inv_v),
    ]
    loads = [pltpu.make_async_copy(x, y, lsem.at[k]) for k, (x, y) in enumerate(wanted)]
    load_lists, load_res, load_pmap, load_crows, load_basis, load_stiff, load_inv = loads
    barrier = pltpu.get_barrier_semaphore()
    for o in range(1, gx):
        pl.semaphore_signal(barrier, inc=1, device_id=(lax.rem(a + o, gx), b), device_id_type=MESH)
    for o in range(1, gy):
        pl.semaphore_signal(barrier, inc=1, device_id=(a, lax.rem(b + o, gy)), device_id_type=MESH)

    for load in loads:
        load.start()

    up = [(a + 1, b), (a - 1, b), (a, b + 1), (a, b - 1)]
    has_up = [a < gx - 1, a > 0, b < gy - 1, b > 0]
    down = [up[p ^ 1] for p in range(4)]
    has_down = [has_up[p ^ 1] for p in range(4)]
    finish = []

    def send(copies, conds, wait):
        for p in (2, 3, 0, 1):
            @pl.when(conds[p])
            def _(p=p):
                for c in copies(p):
                    getattr(c, wait)()

    def trade(copies, forward):
        to, fro = (has_up, has_down) if forward else (has_down, has_up)
        send(copies, to, "start")
        finish.append(lambda: send(copies, to, "wait_send"))
        return lambda: send(copies, fro, "wait_recv")

    def remote(src, dst, s, r, dev):
        return pltpu.make_async_remote_copy(
            src_ref=src, dst_ref=dst, send_sem=s, recv_sem=r, device_id=dev, device_id_type=MESH
        )

    load_lists.wait()
    rows = fiota((own, ov), 0)
    lists = lists_ref[...].astype(F32)
    for h in range(2):
        two = [jnp.where(rows == lists[p ^ 1 : (p ^ 1) + 1], 1.0, 0.0) for p in (2 * h, 2 * h + 1)]
        both = jnp.concatenate(two, axis=1)
        sel[:, 2 * ov * h : 2 * ov * (h + 1)] = both.astype(BF16)
        selt[2 * ov * h : 2 * ov * (h + 1), :] = both.T.astype(BF16)

    for p in range(4):
        at = own + p * ov

        @pl.when(jnp.logical_not(has_down[p]))
        def _(p=p, at=at):
            for t in range(2):
                sub[t, at : at + ov, :] = jnp.zeros((ov, nv), BF16)
                hr[t, p] = jnp.zeros(hr.shape[2:], BF16)

        @pl.when(jnp.logical_not(has_up[p]))
        def _(p=p):
            for t in range(2):
                backr[t, p * ov : (p + 1) * ov, :] = jnp.zeros((ov, nv), BF16)
            sext[(p + 1) * kw : (p + 2) * kw, :] = jnp.zeros((kw, kd), F32)
            brecv[p * kw : (p + 1) * kw, :] = jnp.zeros((kw, 4 * ov), F32)

        @pl.when(jnp.logical_not(has_down[p]))
        def _(p=p):
            cmat[own + p * halo : own + (p + 1) * halo, :] = jnp.zeros((halo, kd), BF16)

    sext[5 * kw :, :] = jnp.zeros((sext.shape[0] - 5 * kw, kd), F32)

    load_res.wait()

    def gather(t, src):
        value = src[...].astype(BF16)
        sub[t, :own, :] = value
        outs[t] = dot(selt[...], value).astype(BF16)

    gather(0, res_v)
    pl.semaphore_wait(barrier, gx + gy - 2)

    def start_margins(t):
        return trade(
            lambda p: [remote(outs.at[t, pl.ds(p * ov, ov)], sub.at[t, pl.ds(own + p * ov, ov)],
                              nsem_s.at[t, 0, p], nsem_r.at[t, 0, p], up[p])],
            True,
        )

    wait_margins = start_margins(0)

    load_pmap.wait()
    load_crows.wait()
    load_basis.wait()
    wide = min(kd, 256)
    n = gx * gy
    pmf = jnp.broadcast_to(pmap_ref[...].astype(F32), (8, n))

    def order(c, _):
        q = fiota((1, wide), 1) + (c * wide).astype(F32)
        slot = fdiv(q, kw)
        slab = fdiv(slot, gx)
        dev = (slot - slab * gx) * gy + slab
        pick = jnp.where(fiota((n, wide), 0) == dev, 1.0, 0.0)
        place = dot(pmf, pick, precision=HIGH)[0:1] * kw + (q - slot * kw)
        perm = jnp.where(fiota((kd, wide), 0) == place, 1.0, 0.0).astype(BF16)
        sext[0:kw, pl.ds(pl.multiple_of(c * wide, wide), wide)] = dot(crows_ref[...], perm)
        return 0

    lax.fori_loop(jnp.int32(0), jnp.int32(kd // wide), order, 0)
    bsend[...] = basis_ref[:, own:].astype(F32)
    wait_coarse = trade(
        lambda p: [
            remote(sext.at[pl.ds(0, kw)], sext.at[pl.ds((p + 1) * kw, kw)], csem_s.at[0, p], csem_r.at[0, p], down[p]),
            remote(bsend, brecv.at[pl.ds(p * kw, kw)], csem_s.at[1, p], csem_r.at[1, p], down[p]),
        ],
        False,
    )

    load_stiff.wait()
    r1 = fiota((layer, cy), 0)
    first = fdiv(r1, cy)
    mine = jnp.where(fiota((layer, cx), 1) == fdiv(fiota((layer, cx), 0), cy), 1.0, 0.0)
    spread = dot(mine, stiff_ref[...], precision=HIGH)
    spread = jnp.where(fiota((layer, cy), 1) == r1 - first * cy, spread, 0.0)
    diag[...] = jnp.broadcast_to(4.0 + jnp.sum(spread, axis=1, keepdims=True), (layer, nv))
    rr = fiota((layer, nv), 0)
    second = rr - fdiv(rr, cy) * cy
    m_lo[...] = jnp.where(second == 0.0, 0.0, 1.0)
    m_hi[...] = jnp.where(second == cy - 1.0, 0.0, 1.0)

    def layer_rows(ref, p):
        if p >= 2:
            return ref[pl.ds((cy - 1) * (3 - p), comps * cx, stride=cy), :]
        skip = (layer - cy) * (1 - p)
        return jnp.concatenate([ref[c * layer + skip : c * layer + skip + cy, :] for c in range(comps)], axis=0)

    def operate(x_ref, dst, src):
        zero = jnp.zeros((cy, nv), F32)
        for c in range(comps):
            at = pl.ds(c * layer, layer)
            x = x_ref[at, :]
            beside = jnp.concatenate([zero, x[:-cy]], axis=0) + jnp.concatenate([x[cy:], zero], axis=0)
            beside += pltpu.roll(x, 1, 0) * m_lo[...] + pltpu.roll(x, layer - 1, 0) * m_hi[...]
            value = beside - diag[...] * x
            dst[at, :] = value if src is None else src[at, :] + value

    def add_layers(dst, around):
        for c in range(comps):
            base = c * layer
            dst[base : base + cy, :] += around(0)[c * cy : (c + 1) * cy]
            dst[base + layer - cy : base + layer, :] += around(1)[c * cy : (c + 1) * cy]
        low = pl.ds(0, comps * cx, stride=cy)
        high = pl.ds(cy - 1, comps * cx, stride=cy)
        dst[low, :] = dst[low, :] + around(2)
        dst[high, :] = dst[high, :] + around(3)

    wait_edges = []

    def correct(t, src, dst, wait_margins):
        if t == 0:
            load_inv.wait()
        part = dot(inv_v[:, :own], sub[t, :own, :])
        cpart = dot(basis_ref[:, :own], sub[t, :own, :])
        wait_margins()
        edge = sub[t, own:, :]
        cin = cpart + dot(basis_ref[:, own:], edge)
        allbuf[t, b, a] = cin.astype(BF16)

        def stage1(o, dev, slot):
            ref = allbuf.at[t, b, slot]
            return remote(ref, ref, g1s.at[t, o], g1r.at[t, o], (dev, b))

        def stage2(o, dev, slot):
            ref = allbuf.at[t, slot]
            return remote(ref, ref, g2s.at[t, o], g2r.at[t, o], (a, dev))

        for o in range(1, gx):
            stage1(o, lax.rem(a + o, gx), a).start()
        backs[t] = (part[own:] + dot(inv_v[own:, own:], edge)).astype(BF16)
        wait_back = trade(
            lambda p: [remote(backs.at[t, pl.ds(p * ov, ov)], backr.at[t, pl.ds(p * ov, ov)],
                              nsem_s.at[t, 1, p], nsem_r.at[t, 1, p], down[p])],
            False,
        )
        xs[...] = part[:own] + dot(inv_v[:own, own:], edge)
        if t == 0:
            wait_coarse()
            rb = fdiv(fiota((4 * kw, 4 * ov), 0), kw)
            cb = fdiv(fiota((4 * kw, 4 * ov), 1), ov)
            margins = jnp.where(rb == cb, brecv[...], 0.0).astype(BF16)
            below = dot(margins, selt[...])
            rest = jnp.zeros((sext.shape[0] - 5 * kw, own), F32)
            ext = jnp.concatenate([basis_ref[:, :own].astype(F32), below, rest], axis=0)
            bextf[...] = ext.T
            edges = jnp.concatenate([layer_rows(bextf, p) for p in range(4)], axis=0).astype(BF16)

            def build(c, _):
                at = pl.ds(pl.multiple_of(c * wide, wide), wide)
                part_s = sext[:, at].astype(BF16)
                csend[:, at] = dot(edges, part_s).astype(BF16)
                return 0

            lax.fori_loop(jnp.int32(0), jnp.int32(kd // wide), build, 0)
            wait_edges.append(trade(
                lambda p: [remote(csend.at[pl.ds(p * halo, halo)], cmat.at[pl.ds(own + p * halo, halo)],
                                  csem_s.at[2, p], csem_r.at[2, p], up[p])],
                True,
            ))
        for o in range(1, gx):
            stage1(o, lax.rem(a + o, gx), lax.rem(a + (gx - o), gx)).wait_recv()
        for o in range(1, gy):
            stage2(o, lax.rem(b + o, gy), b).start()
        wait_back()
        xs[...] += dot(sel[...], backr[t])

        for p in range(4):
            hs[t, p, : hrows[p], :] = layer_rows(xs, p).astype(hs.dtype)
        wait_halo = trade(
            lambda p: [remote(hs.at[t, p], hr.at[t, p], nsem_s.at[t, 2, p], nsem_r.at[t, 2, p], up[p])],
            True,
        )
        operate(xs, dst, src)
        if t == 0:
            wait_edges[0]()
            bext = bextf[...].astype(BF16)

            def fill(c, _):
                at = pl.ds(pl.multiple_of(c * nv, nv), nv)
                value = dot(bext, sext[:, at].astype(BF16))
                cmat[:own, at] = value.astype(BF16)
                sol_ref[...] = value
                operate(sol_ref, fin_ref, None)
                add_layers(fin_ref, lambda p: cmat[own + p * halo : own + p * halo + hrows[p], at].astype(F32))
                acmat[:, at] = fin_ref[...].astype(BF16)
                return 0

            lax.fori_loop(jnp.int32(0), jnp.int32(kd // nv), fill, 0)
        wait_halo()
        add_layers(dst, lambda p: hr[t, p, : hrows[p], :].astype(F32))
        for o in range(1, gy):
            stage2(o, lax.rem(b + o, gy), lax.rem(b + (gy - o), gy)).wait_recv()
        gathered = allbuf[t].astype(F32).reshape(kd, nv).astype(BF16)
        dst[...] += dot(acmat[...], gathered)

        def done():
            for o in range(1, gx):
                stage1(o, lax.rem(a + o, gx), a).wait_send()
            for o in range(1, gy):
                stage2(o, lax.rem(b + o, gy), b).wait_send()

        finish.append(done)

        return gathered

    gathered = correct(0, res_v, mid, wait_margins)
    gather(1, mid)
    wait_margins = start_margins(1)
    sol_ref[...] = xs[...] + dot(cmat[:own, :], gathered)
    gathered = correct(1, mid, fin_ref, wait_margins)
    sol_ref[...] += xs[...] + dot(cmat[:own, :], gathered)
    for end in finish:
        end()


def solution(mesh):
    gx, gy = mesh.shape["gx"], mesh.shape["gy"]

    def per_device(residual, stiffness, local_inverse, coarse_basis, coarse_rows, send_rows, partition_map):
        comps, cx, cy, nv = residual.shape
        own, layer = comps * cx * cy, cx * cy
        m = local_inverse.shape[-1]
        ov = send_rows.shape[-1]
        kw, kd = coarse_rows.shape[-2:]
        halo = comps * max(cx, cy)
        lanes = -(-5 * kw // 128) * 128
        vm = pl.BlockSpec(memory_space=pltpu.VMEM)
        anywhere = pl.BlockSpec(memory_space=pl.ANY)
        dma = pltpu.SemaphoreType.DMA
        out = pl.pallas_call(
            functools.partial(kernel, gx, gy, (comps, cx, cy, nv)),
            out_shape=[pltpu.VMEM((own, nv), F32)] * 2,
            in_specs=[anywhere] * 7,
            out_specs=[vm, vm],
            scratch_shapes=[
                pltpu.VMEM((own, nv), F32),
                pltpu.VMEM((cx, cy), F32),
                pltpu.VMEM((m, m), BF16),
                pltpu.VMEM((kw, m), BF16),
                pltpu.VMEM((kw, kd), BF16),
                pltpu.VMEM((4, ov), jnp.int32),
                pltpu.VMEM((1, gx * gy), jnp.int32),
                pltpu.VMEM((2, m, nv), BF16),
                pltpu.VMEM((own, 4 * ov), BF16),
                pltpu.VMEM((4 * ov, own), BF16),
                pltpu.VMEM((2, 4 * ov, nv), BF16),
                pltpu.VMEM((2, 4 * ov, nv), BF16),
                pltpu.VMEM((2, 4 * ov, nv), BF16),
                pltpu.VMEM((2, 4, halo, nv), BF16),
                pltpu.VMEM((2, 4, halo, nv), BF16),
                pltpu.VMEM((2, gy, gx, kw, nv), BF16),
                pltpu.VMEM((lanes, kd), F32),
                pltpu.VMEM((kw, m - own), F32),
                pltpu.VMEM((4 * kw, m - own), F32),
                pltpu.VMEM((own, lanes), F32),
                pltpu.VMEM((own + 4 * halo, kd), BF16),
                pltpu.VMEM((own, kd), BF16),
                pltpu.VMEM((4 * halo, kd), BF16),
                pltpu.VMEM((layer, nv), F32),
                pltpu.VMEM((layer, nv), F32),
                pltpu.VMEM((layer, nv), F32),
                pltpu.VMEM((own, nv), F32),
                pltpu.VMEM((own, nv), F32),
                dma((7,)),
                dma((2, 3, 4)),
                dma((2, 3, 4)),
                dma((3, 4)),
                dma((3, 4)),
                dma((2, gx)),
                dma((2, gx)),
                dma((2, gy)),
                dma((2, gy)),
            ],
            compiler_params=pltpu.CompilerParams(collective_id=0, has_side_effects=True),
        )(
            residual.reshape(own, nv),
            stiffness,
            local_inverse[0, 0],
            coarse_basis[0, 0],
            coarse_rows[0, 0],
            send_rows[0, 0],
            partition_map.reshape(1, -1),
        )
        return tuple(o.reshape(residual.shape) for o in out)

    placed = (
        P(None, "gx", "gy", None),
        P("gx", "gy"),
        P("gx", "gy", None, None),
        P("gx", "gy", None, None),
        P("gx", "gy", None, None),
        P("gx", "gy", None, None),
        P(),
    )
    return jax.shard_map(
        per_device,
        mesh=mesh,
        in_specs=placed,
        out_specs=(P(None, "gx", "gy", None), P(None, "gx", "gy", None)),
        check_vma=False,
    )
```

profile of v0, /device:TPU:0, one launch (start us, length us, event | category | flops | bytes accessed | tf_op | source)
XLA Modules:
  0.0 31.2 jit_solution(15029759236386915702)
XLA Ops:
  0.6 29.0 %shard_map.86 = (f32[768,128]{1,0:T(8,128)S(1)}, f32[768,128]{1,0:T(8,128)S(1)}) custom-call(f32[768,128]{1,0:T(8,128)} %bitcast.11, f32[16,16]{1,0:T(8,128)} %stiff_hbm.1, bf16[1024,1024]{1,0:T(8,128)(2,1)} %bitcast.10, bf16[8,1024]{1,0:T(8,128)(2,1)} %bitcast.12, bf16[8,256]{1,0:T(8,128)(2,1)} %bitcast.13, s32[4,64]{1,0:T(4,128)} %bitcast.14, s32[1,32]{1,0:T(1,128)} %bitcast.15), custom_call_target="tpu_custom_call" | custom-call | tf_op jit(solution)/shard_map/pallas_call | solution.py:327
  29.7 0.7 %copy.11 = f32[3,16,16,128]{3,2,1,0:T(8,128)} copy(f32[3,16,16,128]{3,2,1,0:T(8,128)S(1)} %bitcast.9) | data formatting | bytes 786432
  30.4 0.7 %copy.12 = f32[3,16,16,128]{3,2,1,0:T(8,128)} copy(f32[3,16,16,128]{3,2,1,0:T(8,128)S(1)} %bitcast.8) | data formatting | bytes 786432
where the time goes:
time: 31.4 us; the launch traced here: 31.2 us
  Pallas kernels  29 us (92%)
  local copies, waits for them, and re-layouts  1.49 us (5%)
  between operations  0.64 us (2%)
    pallas_call x1, Pallas kernels, per_device(): pl.pallas_call(functools.partial(kernel, gx, gy, (comps, cx, cy, nv)), ou...  29 us
    unnamed x2, local copies, waits for them, and re-layouts  1.49 us

commit v1 on v0

--- a/solution.py
+++ b/solution.py
@@ -33,17 +33,20 @@
     gx, gy, dims,
     res_hbm, stiff_hbm, inv_hbm, basis_hbm, crows_hbm, lists_hbm, pmap_hbm,
     sol_ref, fin_ref,
-    res_v, stiff_ref, inv_v, basis_ref, crows_ref, lists_ref, pmap_ref, sub, sel, selt, outs, backs, backr, hs, hr, allbuf,
+    res_v, stiff_ref, inv_v, basis_ref, crows_ref, lists_ref, pmap_ref, sub, sel, near, outs, msg_s, msg_r,
+    dsend, drecv, qs, qr, gmat, pmat, gp, allbuf,
     sext, bsend, brecv, bextf, cmat, acmat, csend, diag, m_lo, m_hi, xs, mid,
-    lsem, nsem_s, nsem_r, csem_s, csem_r, g1s, g1r, g2s, g2r,
+    lsem, nsem_s, nsem_r, dsem_s, dsem_r, csem_s, csem_r, gs, gr,
 ):
     comps, cx, cy, nv = dims
-    halo = hr.shape[2]
+    halo = comps * max(cx, cy)
     hrows = (comps * cy, comps * cy, comps * cx, comps * cx)
     own = comps * cx * cy
     layer = cx * cy
     ov = lists_ref.shape[1]
     kw, kd = crows_ref.shape
+    n = gx * gy
+    dr = drecv.shape[1] // 4
     a = lax.axis_index("gx")
     b = lax.axis_index("gy")
 
@@ -53,19 +56,54 @@
     ]
     loads = [pltpu.make_async_copy(x, y, lsem.at[k]) for k, (x, y) in enumerate(wanted)]
     load_lists, load_res, load_pmap, load_crows, load_basis, load_stiff, load_inv = loads
-    barrier = pltpu.get_barrier_semaphore()
-    for o in range(1, gx):
-        pl.semaphore_signal(barrier, inc=1, device_id=(lax.rem(a + o, gx), b), device_id_type=MESH)
-    for o in range(1, gy):
-        pl.semaphore_signal(barrier, inc=1, device_id=(a, lax.rem(b + o, gy)), device_id_type=MESH)
-
     for load in loads:
         load.start()
+
+    def flip(x, k):
+        y, bit = x, 1
+        while bit <= k:
+            if k & bit:
+                y = y + bit * (1 - 2 * lax.rem(lax.div(x, bit), 2))
+            bit *= 2
+        return y
+
+    paired = gx & (gx - 1) == 0 and gy & (gy - 1) == 0
+    others = [(i, j) for i in range(gx) for j in range(gy) if i or j]
+    if paired:
+        others.sort(key=lambda o: -((o[0] >> 1) + bin(o[1]).count("1") + 0.4 * (o[0] & 1)))
+        to_a = [flip(a, i) for i in range(gx)]
+        to_b = [flip(b, j) for j in range(gy)]
+    else:
+        to_a = [lax.rem(a + i, gx) for i in range(gx)]
+        to_b = [lax.rem(b + j, gy) for j in range(gy)]
+
+    def each_other(act):
+        if n <= 64:
+            for i, j in others:
+                act((to_a[i], to_b[j]))
+            return
+
+        def row(i, _):
+            ai = lax.rem(a + i, gx)
+            for j in range(1, gy):
+                act((ai, lax.rem(b + j, gy)))
+            pl.when(i > 0)(lambda: act((ai, b)))
+            return 0
+
+        lax.fori_loop(jnp.int32(0), jnp.int32(gx), row, 0)
+
+    barrier = pltpu.get_barrier_semaphore()
+    each_other(lambda dev: pl.semaphore_signal(barrier, inc=1, device_id=dev, device_id_type=MESH))
 
     up = [(a + 1, b), (a - 1, b), (a, b + 1), (a, b - 1)]
     has_up = [a < gx - 1, a > 0, b < gy - 1, b > 0]
     down = [up[p ^ 1] for p in range(4)]
     has_down = [has_up[p ^ 1] for p in range(4)]
+    corner = [(1, 1), (-1, -1), (1, -1), (-1, 1)]
+    cdev = [(a + sx, b + sy) for sx, sy in corner]
+    has_c = [
+        jnp.logical_and(has_up[0 if sx > 0 else 1], has_up[2 if sy > 0 else 3]) for sx, sy in corner
+    ]
     finish = []
 
     def send(copies, conds, wait):
@@ -75,8 +113,7 @@
                 for c in copies(p):
                     getattr(c, wait)()
 
-    def trade(copies, forward):
-        to, fro = (has_up, has_down) if forward else (has_down, has_up)
+    def trade(copies, to, fro):
         send(copies, to, "start")
         finish.append(lambda: send(copies, to, "wait_send"))
         return lambda: send(copies, fro, "wait_recv")
@@ -86,14 +123,59 @@
             src_ref=src, dst_ref=dst, send_sem=s, recv_sem=r, device_id=dev, device_id_type=MESH
         )
 
+    wide_grid = 4 * max(cx, cy)
+
+    def code(c, i, j):
+        return (c * wide_grid + (i + cx)) * wide_grid + (j + cy)
+
     load_lists.wait()
-    rows = fiota((own, ov), 0)
     lists = lists_ref[...].astype(F32)
-    for h in range(2):
-        two = [jnp.where(rows == lists[p ^ 1 : (p ^ 1) + 1], 1.0, 0.0) for p in (2 * h, 2 * h + 1)]
-        both = jnp.concatenate(two, axis=1)
-        sel[:, 2 * ov * h : 2 * ov * (h + 1)] = both.astype(BF16)
-        selt[2 * ov * h : 2 * ov * (h + 1), :] = both.T.astype(BF16)
+    columns = lists.T
+    for p in range(4):
+        count = 2 * hrows[p]
+        q = fiota((1, count), 1)
+        if p < 2:
+            c = fdiv(q, 2 * cy)
+            row = c * layer + (layer - 2 * cy) * (1 - p) + (q - c * 2 * cy)
+        else:
+            second = jnp.where(q >= comps * cx, 1.0, 0.0)
+            row = (q - second * (comps * cx)) * cy + (cy - 2) * (3 - p) + second
+        hit = jnp.broadcast_to(columns[:, (p ^ 1) : (p ^ 1) + 1], (ov, count)) == jnp.broadcast_to(row, (ov, count))
+        near[p, :, :count] = jnp.where(hit, 1.0, 0.0).astype(BF16)
+
+    lc = fdiv(lists, layer)
+    li = fdiv(lists - lc * layer, cy)
+    lj = lists - lc * layer - li * cy
+    for p, (dx, dy) in enumerate(((-1, 0), (1, 0), (0, -1), (0, 1))):
+        mine = code(lc, li + dx * cx, lj + dy * cy)[(p ^ 1) : (p ^ 1) + 1]
+        pair = [mine, jnp.zeros_like(mine)]
+        qs[p] = jnp.broadcast_to(jnp.concatenate(pair if p % 2 == 0 else pair[::-1], axis=1), (8, 2 * ov))
+
+    load_res.wait()
+
+    def gather(t, src):
+        for p in range(4):
+            if p < 2:
+                skip = (layer - 2 * cy) * (1 - p)
+                rows = [src[c * layer + skip : c * layer + skip + 2 * cy, :] for c in range(comps)]
+            else:
+                rows = [src[pl.ds((cy - 2) * (3 - p) + k, comps * cx, stride=cy), :] for k in range(2)]
+            rows = jnp.concatenate(rows, axis=0).astype(BF16)
+            outs[t, p * ov : (p + 1) * ov, :] = dot(near[p, :, : 2 * hrows[p]], rows).astype(BF16)
+
+    gather(0, res_v)
+    pl.semaphore_wait(barrier, n - 1)
+    wait_q = trade(lambda p: [remote(qs.at[p], qr.at[p], csem_s.at[3, p], csem_r.at[3, p], up[p])], has_up, has_down)
+
+    def start_margins(t):
+        return trade(
+            lambda p: [remote(outs.at[t, pl.ds(p * ov, ov)], sub.at[t, pl.ds(own + p * ov, ov)],
+                              nsem_s.at[t, 0, p], nsem_r.at[t, 0, p], up[p])],
+            has_up, has_down,
+        )
+
+    wait_margins = start_margins(0)
+    sub[0, :own, :] = res_v[...].astype(BF16)
 
     for p in range(4):
         at = own + p * ov
@@ -102,45 +184,26 @@
         def _(p=p, at=at):
             for t in range(2):
                 sub[t, at : at + ov, :] = jnp.zeros((ov, nv), BF16)
-                hr[t, p] = jnp.zeros(hr.shape[2:], BF16)
+                msg_r[t, p] = jnp.zeros(msg_r.shape[2:], BF16)
+            qr[p] = jnp.zeros(qr.shape[1:], F32)
+            cmat[own + p * halo : own + (p + 1) * halo, :] = jnp.zeros((halo, kd), BF16)
 
         @pl.when(jnp.logical_not(has_up[p]))
         def _(p=p):
-            for t in range(2):
-                backr[t, p * ov : (p + 1) * ov, :] = jnp.zeros((ov, nv), BF16)
             sext[(p + 1) * kw : (p + 2) * kw, :] = jnp.zeros((kw, kd), F32)
             brecv[p * kw : (p + 1) * kw, :] = jnp.zeros((kw, 4 * ov), F32)
 
-        @pl.when(jnp.logical_not(has_down[p]))
+        @pl.when(jnp.logical_not(has_c[p ^ 1]))
         def _(p=p):
-            cmat[own + p * halo : own + (p + 1) * halo, :] = jnp.zeros((halo, kd), BF16)
+            for t in range(2):
+                drecv[t, p * dr : (p + 1) * dr, :] = jnp.zeros((dr, nv), BF16)
 
     sext[5 * kw :, :] = jnp.zeros((sext.shape[0] - 5 * kw, kd), F32)
-
-    load_res.wait()
-
-    def gather(t, src):
-        value = src[...].astype(BF16)
-        sub[t, :own, :] = value
-        outs[t] = dot(selt[...], value).astype(BF16)
-
-    gather(0, res_v)
-    pl.semaphore_wait(barrier, gx + gy - 2)
-
-    def start_margins(t):
-        return trade(
-            lambda p: [remote(outs.at[t, pl.ds(p * ov, ov)], sub.at[t, pl.ds(own + p * ov, ov)],
-                              nsem_s.at[t, 0, p], nsem_r.at[t, 0, p], up[p])],
-            True,
-        )
-
-    wait_margins = start_margins(0)
 
     load_pmap.wait()
     load_crows.wait()
     load_basis.wait()
     wide = min(kd, 256)
-    n = gx * gy
     pmf = jnp.broadcast_to(pmap_ref[...].astype(F32), (8, n))
 
     def order(c, _):
@@ -161,8 +224,13 @@
             remote(sext.at[pl.ds(0, kw)], sext.at[pl.ds((p + 1) * kw, kw)], csem_s.at[0, p], csem_r.at[0, p], down[p]),
             remote(bsend, brecv.at[pl.ds(p * kw, kw)], csem_s.at[1, p], csem_r.at[1, p], down[p]),
         ],
-        False,
+        has_down, has_up,
     )
+
+    rows = fiota((own, ov), 0)
+    for h in range(2):
+        two = [jnp.where(rows == lists[p : p + 1], 1.0, 0.0) for p in (2 * h, 2 * h + 1)]
+        sel[:, 2 * ov * h : 2 * ov * (h + 1)] = jnp.concatenate(two, axis=1).astype(BF16)
 
     load_stiff.wait()
     r1 = fiota((layer, cy), 0)
@@ -176,6 +244,43 @@
     m_lo[...] = jnp.where(second == 0.0, 0.0, 1.0)
     m_hi[...] = jnp.where(second == cy - 1.0, 0.0, 1.0)
 
+    def ring_codes(p, lanes):
+        w = fiota((halo, lanes), 0)
+        per = cy if p < 2 else cx
+        c = fdiv(w, per)
+        along = w - c * per
+        i, j = (along * 0.0 + (-1.0, cx)[p % 2], along) if p < 2 else (along, along * 0.0 + (-1.0, cy)[p % 2])
+        return jnp.where(w < hrows[p], code(c, i, j), -1.0)
+
+    def corner_codes(w, sx, sy):
+        g = fdiv(w, 2 * comps)
+        c = fdiv(w - g * (2 * comps), 2)
+        k = w - g * (2 * comps) - 2 * c
+        i = jnp.where(g == 0.0, (sx + 1) * 0.5 * (cx - 1), (sx + 1) * 0.5 * (cx - 1) + sx * (1.0 + k))
+        j = jnp.where(g == 0.0, (sy + 1) * 0.5 * (cy - 1) + sy * (1.0 + k), (sy + 1) * 0.5 * (cy - 1))
+        return c, i, j, g < 2.0
+
+    w = fiota((1, 4 * dr), 1)
+    m = fdiv(w, dr)
+    sx = jnp.where(jnp.logical_or(m == 0.0, m == 2.0), 1.0, -1.0)
+    sy = jnp.where(jnp.logical_or(m == 0.0, m == 3.0), 1.0, -1.0)
+    c, i, j, real = corner_codes(w - m * dr, sx, sy)
+    landed = jnp.where(real, code(c, i - sx * cx, j - sy * cy), -2.0)
+    for p in range(4):
+        at = slice(p * halo, (p + 1) * halo)
+        pmat[at, :] = jnp.where(ring_codes(p, 4 * dr) == landed, 1.0, 0.0).astype(BF16)
+
+    def fill_gmat():
+        for h in range(2):
+            q = (qr[2 * h] + qr[2 * h + 1])[0:1]
+            lanes = slice(2 * ov * h, 2 * ov * (h + 1))
+            for p in range(4):
+                at = slice(p * halo, (p + 1) * halo)
+                gmat[at, lanes] = jnp.where(ring_codes(p, 2 * ov) == q, 1.0, 0.0).astype(BF16)
+                c, i, j, real = corner_codes(fiota((dr, 2 * ov), 0), *corner[p])
+                at = slice(4 * halo + p * dr, 4 * halo + (p + 1) * dr)
+                gmat[at, lanes] = jnp.where(jnp.where(real, code(c, i, j), -1.0) == q, 1.0, 0.0).astype(BF16)
+
     def layer_rows(ref, p):
         if p >= 2:
             return ref[pl.ds((cy - 1) * (3 - p), comps * cx, stride=cy), :]
@@ -203,6 +308,7 @@
         dst[high, :] = dst[high, :] + around(3)
 
     wait_edges = []
+    slot = b * gx + a
 
     def correct(t, src, dst, wait_margins):
         if t == 0:
@@ -212,33 +318,41 @@
         wait_margins()
         edge = sub[t, own:, :]
         cin = cpart + dot(basis_ref[:, own:], edge)
-        allbuf[t, b, a] = cin.astype(BF16)
-
-        def stage1(o, dev, slot):
-            ref = allbuf.at[t, b, slot]
-            return remote(ref, ref, g1s.at[t, o], g1r.at[t, o], (dev, b))
-
-        def stage2(o, dev, slot):
-            ref = allbuf.at[t, slot]
-            return remote(ref, ref, g2s.at[t, o], g2r.at[t, o], (a, dev))
-
-        for o in range(1, gx):
-            stage1(o, lax.rem(a + o, gx), a).start()
-        backs[t] = (part[own:] + dot(inv_v[own:, own:], edge)).astype(BF16)
-        wait_back = trade(
-            lambda p: [remote(backs.at[t, pl.ds(p * ov, ov)], backr.at[t, pl.ds(p * ov, ov)],
-                              nsem_s.at[t, 1, p], nsem_r.at[t, 1, p], down[p])],
-            False,
+        allbuf[t, slot] = cin.astype(BF16)
+        here = allbuf.at[t, slot]
+        each_other(lambda dev: remote(here, here, gs.at[t], gr.at[t], dev).start())
+        rest = allbuf.at[t, pl.ds(0, n - 1)]
+        gathering = remote(rest, rest, gs.at[t], gr.at[t], (to_a[0], to_b[1]))
+
+        pm = (part[own:] + dot(inv_v[own:, own:], edge)).astype(BF16)
+        if t == 0:
+            wait_q()
+            fill_gmat()
+        gp[...] = dot(gmat[...], pm)
+        dsend[t] = gp[4 * halo :, :].astype(BF16)
+        wait_corners = trade(
+            lambda p: [remote(dsend.at[t, pl.ds(p * dr, dr)], drecv.at[t, pl.ds(p * dr, dr)],
+                              dsem_s.at[t, p], dsem_r.at[t, p], cdev[p])],
+            has_c, [has_c[p ^ 1] for p in range(4)],
         )
         xs[...] = part[:own] + dot(inv_v[:own, own:], edge)
+        for p in range(4):
+            msg_s[t, p, :ov, :] = pm[(p ^ 1) * ov : ((p ^ 1) + 1) * ov]
+            msg_s[t, p, ov : ov + hrows[p], :] = layer_rows(xs, p).astype(BF16)
+        wait_back = trade(
+            lambda p: [remote(msg_s.at[t, p], msg_r.at[t, p], nsem_s.at[t, 1, p], nsem_r.at[t, 1, p], up[p])],
+            has_up, has_down,
+        )
         if t == 0:
             wait_coarse()
             rb = fdiv(fiota((4 * kw, 4 * ov), 0), kw)
             cb = fdiv(fiota((4 * kw, 4 * ov), 1), ov)
-            margins = jnp.where(rb == cb, brecv[...], 0.0).astype(BF16)
-            below = dot(margins, selt[...])
-            rest = jnp.zeros((sext.shape[0] - 5 * kw, own), F32)
-            ext = jnp.concatenate([basis_ref[:, :own].astype(F32), below, rest], axis=0)
+            margins = jnp.where(rb == cb, brecv[...], 0.0)
+            margins = [pltpu.roll(margins[:, 2 * ov * h : 2 * ov * (h + 1)], ov, 1) for h in range(2)]
+            margins = jnp.concatenate(margins, axis=1).astype(BF16)
+            below = lax.dot_general(margins, sel[...], (((1,), (1,)), ((), ())), preferred_element_type=F32)
+            zeros = jnp.zeros((sext.shape[0] - 5 * kw, own), F32)
+            ext = jnp.concatenate([basis_ref[:, :own].astype(F32), below, zeros], axis=0)
             bextf[...] = ext.T
             edges = jnp.concatenate([layer_rows(bextf, p) for p in range(4)], axis=0).astype(BF16)
 
@@ -252,22 +366,19 @@
             wait_edges.append(trade(
                 lambda p: [remote(csend.at[pl.ds(p * halo, halo)], cmat.at[pl.ds(own + p * halo, halo)],
                                   csem_s.at[2, p], csem_r.at[2, p], up[p])],
-                True,
+                has_up, has_down,
             ))
-        for o in range(1, gx):
-            stage1(o, lax.rem(a + o, gx), lax.rem(a + (gx - o), gx)).wait_recv()
-        for o in range(1, gy):
-            stage2(o, lax.rem(b + o, gy), b).start()
         wait_back()
-        xs[...] += dot(sel[...], backr[t])
-
-        for p in range(4):
-            hs[t, p, : hrows[p], :] = layer_rows(xs, p).astype(hs.dtype)
-        wait_halo = trade(
-            lambda p: [remote(hs.at[t, p], hr.at[t, p], nsem_s.at[t, 2, p], nsem_r.at[t, 2, p], up[p])],
-            True,
-        )
+        backs = jnp.concatenate([msg_r[t, p, :ov, :] for p in range(4)], axis=0)
+        xs[...] += dot(sel[...], backs)
         operate(xs, dst, src)
+        wait_corners()
+        gp[: 4 * halo, :] += dot(pmat[...], drecv[t])
+
+        def around(p):
+            return msg_r[t, p, ov : ov + hrows[p], :].astype(F32) + gp[p * halo : p * halo + hrows[p], :]
+
+        add_layers(dst, around)
         if t == 0:
             wait_edges[0]()
             bext = bextf[...].astype(BF16)
@@ -283,26 +394,16 @@
                 return 0
 
             lax.fori_loop(jnp.int32(0), jnp.int32(kd // nv), fill, 0)
-        wait_halo()
-        add_layers(dst, lambda p: hr[t, p, : hrows[p], :].astype(F32))
-        for o in range(1, gy):
-            stage2(o, lax.rem(b + o, gy), lax.rem(b + (gy - o), gy)).wait_recv()
+        gathering.wait_recv()
         gathered = allbuf[t].astype(F32).reshape(kd, nv).astype(BF16)
         dst[...] += dot(acmat[...], gathered)
-
-        def done():
-            for o in range(1, gx):
-                stage1(o, lax.rem(a + o, gx), a).wait_send()
-            for o in range(1, gy):
-                stage2(o, lax.rem(b + o, gy), b).wait_send()
-
-        finish.append(done)
-
+        finish.append(gathering.wait_send)
         return gathered
 
     gathered = correct(0, res_v, mid, wait_margins)
     gather(1, mid)
     wait_margins = start_margins(1)
+    sub[1, :own, :] = mid[...].astype(BF16)
     sol_ref[...] = xs[...] + dot(cmat[:own, :], gathered)
     gathered = correct(1, mid, fin_ref, wait_margins)
     sol_ref[...] += xs[...] + dot(cmat[:own, :], gathered)
@@ -321,6 +422,7 @@
         kw, kd = coarse_rows.shape[-2:]
         halo = comps * max(cx, cy)
         lanes = -(-5 * kw // 128) * 128
+        dr = -(-4 * comps // 16) * 16
         vm = pl.BlockSpec(memory_space=pltpu.VMEM)
         anywhere = pl.BlockSpec(memory_space=pl.ANY)
         dma = pltpu.SemaphoreType.DMA
@@ -339,13 +441,18 @@
                 pltpu.VMEM((1, gx * gy), jnp.int32),
                 pltpu.VMEM((2, m, nv), BF16),
                 pltpu.VMEM((own, 4 * ov), BF16),
-                pltpu.VMEM((4 * ov, own), BF16),
+                pltpu.VMEM((4, ov, 2 * halo), BF16),
                 pltpu.VMEM((2, 4 * ov, nv), BF16),
-                pltpu.VMEM((2, 4 * ov, nv), BF16),
-                pltpu.VMEM((2, 4 * ov, nv), BF16),
-                pltpu.VMEM((2, 4, halo, nv), BF16),
-                pltpu.VMEM((2, 4, halo, nv), BF16),
-                pltpu.VMEM((2, gy, gx, kw, nv), BF16),
+                pltpu.VMEM((2, 4, ov + halo, nv), BF16),
+                pltpu.VMEM((2, 4, ov + halo, nv), BF16),
+                pltpu.VMEM((2, 4 * dr, nv), BF16),
+                pltpu.VMEM((2, 4 * dr, nv), BF16),
+                pltpu.VMEM((4, 8, 2 * ov), F32),
+                pltpu.VMEM((4, 8, 2 * ov), F32),
+                pltpu.VMEM((4 * halo + 4 * dr, 4 * ov), BF16),
+                pltpu.VMEM((4 * halo, 4 * dr), BF16),
+                pltpu.VMEM((4 * halo + 4 * dr, nv), F32),
+                pltpu.VMEM((2, gx * gy, kw, nv), BF16),
                 pltpu.VMEM((lanes, kd), F32),
                 pltpu.VMEM((kw, m - own), F32),
                 pltpu.VMEM((4 * kw, m - own), F32),
@@ -359,14 +466,14 @@
                 pltpu.VMEM((own, nv), F32),
                 pltpu.VMEM((own, nv), F32),
                 dma((7,)),
-                dma((2, 3, 4)),
-                dma((2, 3, 4)),
-                dma((3, 4)),
-                dma((3, 4)),
-                dma((2, gx)),
-                dma((2, gx)),
-                dma((2, gy)),
-                dma((2, gy)),
+                dma((2, 2, 4)),
+                dma((2, 2, 4)),
+                dma((2, 4)),
+                dma((2, 4)),
+                dma((4, 4)),
+                dma((4, 4)),
+                dma((2,)),
+                dma((2,)),
             ],
             compiler_params=pltpu.CompilerParams(collective_id=0, has_side_effects=True),
         )(

time: 31.4 us -> 28.4 us (0.904)
  Pallas kernels: 29 us -> 26.1 us
    pallas_call x1, Pallas kernels: 29 us -> 26.1 us  [per_device(): pl.pallas_call(functools.partial(kernel, gx, gy, (comps, cx, cy, nv)), ou...]
where the time goes in v1:
time: 28.4 us; the launch traced here: 28.2 us
  Pallas kernels  26.1 us (92%)
  local copies, waits for them, and re-layouts  1.49 us (5%)
  between operations  0.64 us (2%)
    pallas_call x1, Pallas kernels, per_device(): pl.pallas_call(functools.partial(kernel, gx, gy, (comps, cx, cy, nv)), ou...  26.1 us
    unnamed x2, local copies, waits for them, and re-layouts  1.49 us

profile of v1, /device:TPU:0, one launch (start us, length us, event | category | flops | bytes accessed | tf_op | source)
XLA Modules:
  0.0 28.2 jit_solution(16911631808605224907)
XLA Ops:
  0.6 26.1 %shard_map.86 = (f32[768,128]{1,0:T(8,128)S(1)}, f32[768,128]{1,0:T(8,128)S(1)}) custom-call(f32[768,128]{1,0:T(8,128)} %bitcast.11, f32[16,16]{1,0:T(8,128)} %stiff_hbm.1, bf16[1024,1024]{1,0:T(8,128)(2,1)} %bitcast.10, bf16[8,1024]{1,0:T(8,128)(2,1)} %bitcast.12, bf16[8,256]{1,0:T(8,128)(2,1)} %bitcast.13, s32[4,64]{1,0:T(4,128)} %bitcast.14, s32[1,32]{1,0:T(1,128)} %bitcast.15), custom_call_target="tpu_custom_call" | custom-call | tf_op jit(solution)/shard_map/pallas_call | solution.py:429
  26.7 0.7 %copy.11 = f32[3,16,16,128]{3,2,1,0:T(8,128)} copy(f32[3,16,16,128]{3,2,1,0:T(8,128)S(1)} %bitcast.9) | data formatting | bytes 786432
  27.5 0.7 %copy.12 = f32[3,16,16,128]{3,2,1,0:T(8,128)} copy(f32[3,16,16,128]{3,2,1,0:T(8,128)S(1)} %bitcast.8) | data formatting | bytes 786432

commit v2 on v1

v2 whole, which is shorter than its diff:
```python
import functools

import jax
import jax.numpy as jnp
from jax import lax
from jax.experimental import pallas as pl
from jax.experimental.pallas import tpu as pltpu
from jax.sharding import PartitionSpec as P

MESH = pl.DeviceIdType.MESH
F32 = jnp.float32
BF16 = jnp.bfloat16
HIGH = lax.Precision.HIGHEST


def dot(x, y, **kw):
    return jnp.dot(x, y, preferred_element_type=F32, **kw)


def tdot(x, y):
    return lax.dot_general(x, y, (((0,), (0,)), ((), ())), preferred_element_type=F32)


def fiota(shape, axis):
    return lax.broadcasted_iota(jnp.int32, shape, axis).astype(F32)


def fdiv(x, n):
    return jnp.floor((x + 0.5) * (1.0 / n))


def kernel(
    gx, gy, dims,
    res_hbm, stiff_hbm, inv_hbm, basis_hbm, crows_hbm, lists_hbm, pmap_hbm,
    sol_ref, fin_ref,
    res_v, stiff_ref, inv_v, basis_ref, crows_ref, lists_ref, pmap_ref, sub, sel, near, outs,
    ybuf, ycode, rowc, qb, sb, gmat, mmat, pmat, pmat2, ring, msg_s, dsend, msg2_s, msg2_r, dsend2, drecv2,
    qs, qr, ts, tr, allbuf, ball, sall, sext, bt, bextf, abf, bextb, abextb, am_s, am_r, edge2,
    diag, m_lo, m_hi, xs, mid,
    lsem, nsem_s, nsem_r, dsem_s, dsem_r, csem_s, csem_r, rsem_s, rsem_r, gs, gr,
):
    comps, cx, cy, nv = dims
    halo = comps * max(cx, cy)
    hrows = (comps * cy, comps * cy, comps * cx, comps * cx)
    own = comps * cx * cy
    layer = cx * cy
    ov = lists_ref.shape[1]
    kw, kd = crows_ref.shape
    n = gx * gy
    mrows = msg_s.shape[1]
    crows = mrows - ov - 3 * halo
    dr, dr2 = dsend.shape[1], dsend2.shape[0] // 4
    yedge = 4 * ov
    ymsg = yedge + 4 * halo
    ycorner = ymsg + 4 * mrows
    ny = ybuf.shape[0]
    nine = ball.shape[0]
    lanes = bextf.shape[1]
    a = lax.axis_index("gx")
    b = lax.axis_index("gy")

    wanted = [
        (lists_hbm, lists_ref), (res_hbm, res_v), (pmap_hbm, pmap_ref), (crows_hbm, crows_ref),
        (basis_hbm, basis_ref), (stiff_hbm, stiff_ref), (inv_hbm, inv_v),
    ]
    loads = [pltpu.make_async_copy(x, y, lsem.at[k]) for k, (x, y) in enumerate(wanted)]
    load_lists, load_res, load_pmap, load_crows, load_basis, load_stiff, load_inv = loads
    for load in loads:
        load.start()

    def flip(x, k):
        y, bit = x, 1
        while bit <= k:
            if k & bit:
                y = y + bit * (1 - 2 * lax.rem(lax.div(x, bit), 2))
            bit *= 2
        return y

    paired = gx & (gx - 1) == 0 and gy & (gy - 1) == 0
    others = [(i, j) for i in range(gx) for j in range(gy) if i or j]
    if paired:
        others.sort(key=lambda o: -((o[0] >> 1) + bin(o[1]).count("1") + 0.4 * (o[0] & 1)))
        to_a = [flip(a, i) for i in range(gx)]
        to_b = [flip(b, j) for j in range(gy)]
    else:
        to_a = [lax.rem(a + i, gx) for i in range(gx)]
        to_b = [lax.rem(b + j, gy) for j in range(gy)]

    def each_other(act):
        if n <= 64:
            for i, j in others:
                act((to_a[i], to_b[j]))
            return

        def row(i, _):
            ai = lax.rem(a + i, gx)
            for j in range(1, gy):
                act((ai, lax.rem(b + j, gy)))
            pl.when(i > 0)(lambda: act((ai, b)))
            return 0

        lax.fori_loop(jnp.int32(0), jnp.int32(gx), row, 0)

    barrier = pltpu.get_barrier_semaphore()
    each_other(lambda dev: pl.semaphore_signal(barrier, inc=1, device_id=dev, device_id_type=MESH))

    up = [(a + 1, b), (a - 1, b), (a, b + 1), (a, b - 1)]
    has_up = [a < gx - 1, a > 0, b < gy - 1, b > 0]
    down = [up[p ^ 1] for p in range(4)]
    has_down = [has_up[p ^ 1] for p in range(4)]
    corner = [(1, 1), (-1, -1), (1, -1), (-1, 1)]
    cdev = [(a + sx, b + sy) for sx, sy in corner]
    has_c = [
        jnp.logical_and(has_up[0 if sx > 0 else 1], has_up[2 if sy > 0 else 3]) for sx, sy in corner
    ]
    finish = []

    def send(copies, conds, wait):
        for p in (2, 3, 0, 1):
            @pl.when(conds[p])
            def _(p=p):
                for c in copies(p):
                    getattr(c, wait)()

    def trade(copies, to, fro):
        send(copies, to, "start")
        finish.append(lambda: send(copies, to, "wait_send"))
        return lambda: send(copies, fro, "wait_recv")

    def remote(src, dst, s, r, dev):
        return pltpu.make_async_remote_copy(
            src_ref=src, dst_ref=dst, send_sem=s, recv_sem=r, device_id=dev, device_id_type=MESH
        )

    wide_grid = 4 * max(cx, cy)

    def code(c, i, j):
        return (c * wide_grid + (i + cx)) * wide_grid + (j + cy)

    load_lists.wait()
    lists = lists_ref[...].astype(F32)
    columns = lists.T
    for p in range(4):
        count = 2 * hrows[p]
        q = fiota((1, count), 1)
        if p < 2:
            c = fdiv(q, 2 * cy)
            row = c * layer + (layer - 2 * cy) * (1 - p) + (q - c * 2 * cy)
        else:
            second = jnp.where(q >= comps * cx, 1.0, 0.0)
            row = (q - second * (comps * cx)) * cy + (cy - 2) * (3 - p) + second
        hit = jnp.broadcast_to(columns[:, (p ^ 1) : (p ^ 1) + 1], (ov, count)) == jnp.broadcast_to(row, (ov, count))
        near[p, :, :count] = jnp.where(hit, 1.0, 0.0).astype(BF16)

    lc = fdiv(lists, layer)
    li = fdiv(lists - lc * layer, cy)
    lj = lists - lc * layer - li * cy
    block = fdiv(fiota((1, 4 * ov), 1), ov)

    def in_line(x):
        return jnp.concatenate([x[(p ^ 1) : (p ^ 1) + 1] for p in range(4)], axis=1)

    sides = ((-1, 0), (1, 0), (0, -1), (0, 1))
    for p, (dx, dy) in enumerate(sides):
        line = in_line(code(lc, li + dx * cx, lj + dy * cy))
        qs[p, 0:1, :] = jnp.where(block == p, line, 0.0)
        qs[p, 1:2, :] = line

    load_res.wait()

    def gather(t, src):
        for p in range(4):
            if p < 2:
                skip = (layer - 2 * cy) * (1 - p)
                rows = [src[c * layer + skip : c * layer + skip + 2 * cy, :] for c in range(comps)]
            else:
                rows = [src[pl.ds((cy - 2) * (3 - p) + k, comps * cx, stride=cy), :] for k in range(2)]
            rows = jnp.concatenate(rows, axis=0).astype(BF16)
            outs[t, p * ov : (p + 1) * ov, :] = dot(near[p, :, : 2 * hrows[p]], rows).astype(BF16)

    gather(0, res_v)
    pl.semaphore_wait(barrier, n - 1)

    def start_margins(t):
        return trade(
            lambda p: [
                remote(outs.at[t, pl.ds(p * ov, ov)], sub.at[t, pl.ds(own + p * ov, ov)],
                       nsem_s.at[0, p], nsem_r.at[0, p], up[p]),
                remote(qs.at[p], qr.at[p], csem_s.at[0, p], csem_r.at[0, p], up[p]),
            ],
            has_up, has_down,
        )

    wait_margins = start_margins(0)
    has_cd = [has_c[p ^ 1] for p in range(4)]
    wait_raw = trade(
        lambda p: [
            remote(basis_hbm, ball.at[1 + p], csem_s.at[1, p], csem_r.at[1, p], up[p]),
            remote(crows_hbm, sall.at[1 + p], csem_s.at[2, p], csem_r.at[2, p], up[p]),
        ],
        has_up, has_down,
    )
    wait_raw_c = trade(
        lambda p: [
            remote(basis_hbm, ball.at[5 + p], rsem_s.at[0, p], rsem_r.at[0, p], cdev[p]),
            remote(crows_hbm, sall.at[5 + p], rsem_s.at[1, p], rsem_r.at[1, p], cdev[p]),
        ],
        has_c, has_cd,
    )
    sub[0, :own, :] = res_v[...].astype(BF16)

    for p in range(4):
        @pl.when(jnp.logical_not(has_down[p]))
        def _(p=p):
            sub[0, own + p * ov : own + (p + 1) * ov, :] = jnp.zeros((ov, nv), BF16)
            ybuf[ymsg + p * mrows : ymsg + (p + 1) * mrows, :] = jnp.zeros((mrows, nv), BF16)
            msg2_r[p] = jnp.zeros(msg2_r.shape[1:], BF16)
            qr[p] = jnp.zeros(qr.shape[1:], F32)
            tr[p] = jnp.zeros(tr.shape[1:], F32)
            am_r[p * ov : (p + 1) * ov, :] = jnp.zeros((ov, kd), BF16)
            ball[1 + p] = jnp.zeros(ball.shape[1:], BF16)
            sall[1 + p] = jnp.zeros(sall.shape[1:], BF16)

        @pl.when(jnp.logical_not(has_cd[p]))
        def _(p=p):
            ybuf[ycorner + p * dr : ycorner + (p + 1) * dr, :] = jnp.zeros((dr, nv), BF16)
            drecv2[p * dr2 : (p + 1) * dr2, :] = jnp.zeros((dr2, nv), BF16)
            ball[5 + p] = jnp.zeros(ball.shape[1:], BF16)
            sall[5 + p] = jnp.zeros(sall.shape[1:], BF16)

    if ny > ycorner + 4 * dr:
        ybuf[ycorner + 4 * dr :, :] = jnp.zeros((ny - ycorner - 4 * dr, nv), BF16)

    load_stiff.wait()
    r1 = fiota((layer, cy), 0)
    first = fdiv(r1, cy)
    mine = jnp.where(fiota((layer, cx), 1) == fdiv(fiota((layer, cx), 0), cy), 1.0, 0.0)
    spread = dot(mine, stiff_ref[...], precision=HIGH)
    spread = jnp.where(fiota((layer, cy), 1) == r1 - first * cy, spread, 0.0)
    diag[...] = jnp.broadcast_to(4.0 + jnp.sum(spread, axis=1, keepdims=True), (layer, nv))
    rr = fiota((layer, nv), 0)
    second = rr - fdiv(rr, cy) * cy
    m_lo[...] = jnp.where(second == 0.0, 0.0, 1.0)
    m_hi[...] = jnp.where(second == cy - 1.0, 0.0, 1.0)

    cells = jnp.where(fiota((layer, 4 * ov), 0) == in_line(li * cy + lj), 1.0, 0.0)
    at_cells = lax.dot_general(
        diag[...], cells, (((0,), (0,)), ((), ())), precision=HIGH, preferred_element_type=F32
    )[0:8]
    for p in range(4):
        ts[p] = jnp.where(jnp.broadcast_to(block, (8, 4 * ov)) == p, at_cells, 0.0)
    wait_t = trade(
        lambda p: [remote(ts.at[p], tr.at[p], csem_s.at[3, p], csem_r.at[3, p], up[p])], has_up, has_down
    )

    def edge_cells(w, p, depth, outside):
        per = cy if p < 2 else cx
        c = fdiv(w, per)
        along = w - c * per
        size = cx if p < 2 else cy
        if outside:
            off = along * 0.0 + (-1.0 - depth, size + depth)[p % 2]
        else:
            off = along * 0.0 + (size - 1.0 - depth, 1.0 * depth)[p % 2]
        return (c, off, along, w < hrows[p]) if p < 2 else (c, along, off, w < hrows[p])

    def beside_cells(w, p):
        v = fdiv(w, 3 * comps)
        u = 1.0 - 2.0 * v
        c = fdiv(w - v * (3 * comps), 3)
        kk = w - v * (3 * comps) - 3 * c
        deep, far = jnp.where(kk == 1.0, 1.0, 0.0), jnp.where(kk == 2.0, 1.0, 0.0)
        size, size2 = (cx, cy) if p < 2 else (cy, cx)
        along = (size - 1.0 - deep) if p % 2 == 0 else deep
        out = jnp.where(v == 0.0, size2 + far, -1.0 - far)
        return (c, along, out, v < 2.0) if p < 2 else (c, out, along, v < 2.0)

    def corner_cells(w, sx, sy):
        ex, ey = (cx - 1.0 if sx > 0 else 0.0), (cy - 1.0 if sy > 0 else 0.0)
        ox, oy = (1.0 * cx if sx > 0 else -1.0), (1.0 * cy if sy > 0 else -1.0)
        g = fdiv(w, 2 * comps)
        depth = fdiv(g, 2)
        kind = g - 2 * depth
        c = fdiv(w - g * (2 * comps), 2)
        k = w - g * (2 * comps) - 2 * c
        i = jnp.where(kind == 0.0, ex - sx * depth, ox + sx * k)
        j = jnp.where(kind == 0.0, oy + sy * k, ey - sy * depth)
        w2 = w - 12 * comps
        c2 = fdiv(w2, 3)
        kk = w2 - 3 * c2
        tail = w2 >= 0.0
        i = jnp.where(tail, ex - sx * jnp.where(kk == 1.0, 1.0, 0.0), i)
        j = jnp.where(tail, ey - sy * jnp.where(kk == 2.0, 1.0, 0.0), j)
        return jnp.where(tail, c2, c), i, j, w < 15 * comps

    nowhere = -16.0 * wide_grid * wide_grid

    def coded(cell, dx=0, dy=0):
        c, i, j, real = cell
        return jnp.where(real, code(c, i - dx * cx, j - dy * cy), nowhere)

    def row_of(count):
        return fiota((1, count), 1)

    tail = []
    for p in range(4):
        c, i, j, real = edge_cells(row_of(halo), p, 0, False)
        if p >= 2:
            real = jnp.logical_and(real, jnp.logical_and(i > 0.0, i < cx - 1.0))
        tail.append(coded((c, i, j, real)))
    for p in range(4):
        ux, uy = -sides[p][0], -sides[p][1]
        tail.append(code(lc, li, lj)[p : p + 1])
        tail += [coded(edge_cells(row_of(halo), p, d, True)) for d in range(3)]
        tail.append(coded(beside_cells(row_of(crows), p), ux, uy))
    for m in range(4):
        tail.append(coded(corner_cells(row_of(dr), *corner[m]), *corner[m]))
    if ny > ycorner + 4 * dr:
        tail.append(jnp.full((1, ny - ycorner - 4 * dr), nowhere, F32))
    ycode[0:1, yedge:] = jnp.concatenate(tail, axis=1)

    def column_of(count):
        return fiota((count, 128), 0)

    rlist = [coded(edge_cells(column_of(halo), p, 0, True)) for p in range(4)]
    rlist += [coded(corner_cells(column_of(dr2), *corner[m])) for m in range(4)]
    rlist += [coded(beside_cells(column_of(crows), p)) for p in range(4)]
    rlist += [coded(corner_cells(column_of(dr - dr2) + dr2, *corner[m])) for m in range(4)]
    rowc[...] = jnp.concatenate(rlist, axis=0)

    def hits(rows, row):
        parts = []
        for at in range(0, row.shape[1], 128):
            piece = row[:, at : at + 128]
            parts.append(jnp.where(rows[:, : piece.shape[1]] == piece, 1.0, 0.0))
        return (jnp.concatenate(parts, axis=1) if len(parts) > 1 else parts[0]).astype(BF16)

    pmat[...] = hits(rowc[: 4 * halo, :], ycode[0:1, ycorner : ycorner + 4 * dr])
    short = [coded(corner_cells(row_of(dr2), *corner[m]), *corner[m]) for m in range(4)]
    pmat2[...] = hits(rowc[: 4 * halo, :], jnp.concatenate(short, axis=1))

    rows = fiota((own, ov), 0)
    for h in range(2):
        two = [jnp.where(rows == lists[p : p + 1], 1.0, 0.0) for p in (2 * h, 2 * h + 1)]
        sel[:, 2 * ov * h : 2 * ov * (h + 1)] = jnp.concatenate(two, axis=1).astype(BF16)

    def layer_rows(ref, p, depth=0):
        if p >= 2:
            return ref[pl.ds(cy - 1 - depth if p == 2 else depth, comps * cx, stride=cy), :]
        skip = layer - cy - depth * cy if p == 0 else depth * cy
        return jnp.concatenate([ref[c * layer + skip : c * layer + skip + cy, :] for c in range(comps)], axis=0)

    def operate(x_ref, dst, src):
        zero = jnp.zeros((cy, nv), F32)
        for c in range(comps):
            at = pl.ds(c * layer, layer)
            x = x_ref[at, :]
            beside = jnp.concatenate([zero, x[:-cy]], axis=0) + jnp.concatenate([x[cy:], zero], axis=0)
            beside += pltpu.roll(x, 1, 0) * m_lo[...] + pltpu.roll(x, layer - 1, 0) * m_hi[...]
            value = beside - diag[...] * x
            dst[at, :] = value if src is None else src[at, :] + value

    def add_layers(dst, around):
        for c in range(comps):
            base = c * layer
            dst[base : base + cy, :] += around(0)[c * cy : (c + 1) * cy]
            dst[base + layer - cy : base + layer, :] += around(1)[c * cy : (c + 1) * cy]
        low = pl.ds(0, comps * cx, stride=cy)
        high = pl.ds(cy - 1, comps * cx, stride=cy)
        dst[low, :] = dst[low, :] + around(2)
        dst[high, :] = dst[high, :] + around(3)

    def ring_side(p):
        return ring[p * halo : p * halo + hrows[p], :]

    slot = b * gx + a

    def start_gather(t, cin):
        allbuf[t, slot] = cin.astype(BF16)
        here = allbuf.at[t, slot]
        each_other(lambda dev: remote(here, here, gs.at[t], gr.at[t], dev).start())
        rest = allbuf.at[t, pl.ds(0, n - 1)]
        gathering = remote(rest, rest, gs.at[t], gr.at[t], (to_a[0], to_b[1]))
        finish.append(gathering.wait_send)

        def arrived():
            gathering.wait_recv()
            return allbuf[t].astype(F32).reshape(kd, nv).astype(BF16)

        return arrived

    load_basis.wait()
    load_inv.wait()
    part = dot(inv_v[:, :own], sub[0, :own, :])
    cpart = dot(basis_ref[:, :own], sub[0, :own, :])
    wait_margins()
    edge = sub[0, own:, :]
    arrived = start_gather(0, cpart + dot(basis_ref[:, own:], edge))
    ycode[0:1, :yedge] = (qr[0] + qr[1] + qr[2] + qr[3])[0:1]
    pm = (part[own:] + dot(inv_v[own:, own:], edge)).astype(BF16)
    ybuf[:yedge, :] = pm
    xs[...] = part[:own] + dot(inv_v[:own, own:], edge)
    ybuf[yedge:ymsg, :] = jnp.concatenate([layer_rows(xs, p) for p in range(4)], axis=0).astype(BF16)
    gmat[...] = hits(rowc[...], ycode[0:1, :ymsg])
    made = dot(gmat[...], ybuf[:ymsg, :])
    ring[...] = made[: 4 * halo]
    made = made[4 * halo :].astype(BF16)
    late = 4 * dr2 + 4 * crows
    for p in range(4):
        msg_s[p, :ov, :] = pm[(p ^ 1) * ov : ((p ^ 1) + 1) * ov]
        for d in range(3):
            msg_s[p, ov + d * halo : ov + d * halo + hrows[p], :] = layer_rows(xs, p, d).astype(BF16)
        msg_s[p, ov + 3 * halo :, :] = made[4 * dr2 + p * crows : 4 * dr2 + (p + 1) * crows]
        dsend[p, :dr2, :] = made[p * dr2 : (p + 1) * dr2]
        dsend[p, dr2:, :] = made[late + p * (dr - dr2) : late + (p + 1) * (dr - dr2)]
    wait_corners = trade(
        lambda p: [remote(dsend.at[p], ybuf.at[pl.ds(ycorner + p * dr, dr)], dsem_s.at[0, p], dsem_r.at[0, p], cdev[p])],
        has_c, has_cd,
    )
    wait_back = trade(
        lambda p: [remote(msg_s.at[p], ybuf.at[pl.ds(ymsg + p * mrows, mrows)], nsem_s.at[1, p], nsem_r.at[1, p], up[p])],
        has_up, has_down,
    )

    load_pmap.wait()
    load_crows.wait()
    wait_raw()
    wait_raw_c()
    ball[0] = basis_ref[...]
    sall[0] = crows_ref[...]
    spare = lanes - nine * kw
    stacked = jnp.concatenate([ball[...].astype(F32).reshape(nine * kw, -1), jnp.zeros((spare, own + 4 * ov), F32)], axis=0)
    bt[...] = stacked.T
    group = fdiv(fiota((1, lanes), 1), kw)

    def of(e, value):
        return jnp.where(group == e, value, 0.0)

    def margin(k):
        return bt[own + k * ov : own + (k + 1) * ov, :]

    theirs = jnp.concatenate([of(1.0 + p, margin(p ^ 1)) for p in range(4)], axis=0).astype(BF16)
    bextf[...] = of(0.0, bt[:own, :]) + dot(sel[...], theirs)
    around_b = jnp.concatenate([of(1.0 + p, layer_rows(bt, p)) for p in range(4)], axis=0)
    around_b += dot(gmat[: 4 * halo, :yedge], of(0.0, bt[own:, :]).astype(BF16))
    for m, (sx, sy) in enumerate(corner):
        ky, py = (0 if sx < 0 else 1), (3 if sy < 0 else 2)
        kx, px = (2 if sy < 0 else 3), (1 if sx < 0 else 0)
        lines = [qr[py, 1:2, ky * ov : (ky + 1) * ov], qr[px, 1:2, kx * ov : (kx + 1) * ov]]
        oh = hits(rowc[: 4 * halo, :], jnp.concatenate(lines, axis=1))
        around_b += dot(oh, of(5.0 + m, jnp.concatenate([margin(ky), margin(kx)], axis=0)).astype(BF16))
    edge2[: 4 * halo, :] = around_b
    operate(bextf, abf, None)
    add_layers(abf, lambda p: edge2[p * halo : p * halo + hrows[p], :])
    bextb[...] = bextf[...].astype(BF16)
    abextb[...] = abf[...].astype(BF16)
    gather(1, abf)

    wide = min(kd, 256)
    pmf = jnp.broadcast_to(pmap_ref[...].astype(F32), (8, n))
    spare_s = jnp.zeros((spare, kd), F32)
    stacked_s = jnp.concatenate([sall[...].astype(F32).reshape(nine * kw, kd), spare_s], axis=0).astype(BF16)

    def order(c, _):
        q = fiota((1, wide), 1) + (c * wide).astype(F32)
        at_slot = fdiv(q, kw)
        slab = fdiv(at_slot, gx)
        dev = (at_slot - slab * gx) * gy + slab
        pick = jnp.where(fiota((n, wide), 0) == dev, 1.0, 0.0)
        place = dot(pmf, pick, precision=HIGH)[0:1] * kw + (q - at_slot * kw)
        perm = jnp.where(fiota((kd, wide), 0) == place, 1.0, 0.0).astype(BF16)
        at = pl.ds(pl.multiple_of(c * wide, wide), wide)
        sext[:, at] = dot(stacked_s, perm).astype(BF16)
        am_s[:, at] = dot(outs[1], sext[:, at]).astype(BF16)
        return 0

    lax.fori_loop(jnp.int32(0), jnp.int32(kd // wide), order, 0)
    wait_am = trade(
        lambda p: [remote(am_s.at[pl.ds(p * ov, ov)], am_r.at[pl.ds(p * ov, ov)], csem_s.at[4, p], csem_r.at[4, p], up[p])],
        has_up, has_down,
    )

    def as_column(line):
        return jnp.broadcast_to(jnp.broadcast_to(line, (8, 4 * ov)).T[:, 0:1], (4 * ov, 128))

    qb[...] = as_column(ycode[0:1, :yedge])
    wait_t()
    sb[...] = as_column((tr[0] + tr[1] + tr[2] + tr[3])[0:1])

    def relate(c, _):
        at = pl.ds(pl.multiple_of(c * 128, 128), 128)
        gap = jnp.abs(ycode[0:1, at] - qb[...])
        mmat[: 4 * ov, at] = jnp.where(gap == 0.0, 1.0, 0.0).astype(BF16)
        mmat[4 * ov :, at] = jnp.where(jnp.logical_or(gap == 1.0, gap == wide_grid), 1.0, 0.0).astype(BF16)
        return 0

    lax.fori_loop(jnp.int32(0), jnp.int32(ny // 128), relate, 0)

    wait_back()
    wait_corners()
    seen = dot(mmat[...], ybuf[...])
    edge2m = sub[0, own:, :].astype(F32) + seen[4 * ov :] - sb[...] * seen[: 4 * ov]
    edge2[: 4 * ov, :] = edge2m
    backs = jnp.concatenate([ybuf[ymsg + p * mrows : ymsg + p * mrows + ov, :] for p in range(4)], axis=0)
    xs[...] += dot(sel[...], backs)
    operate(xs, mid, res_v)
    ring[...] += dot(pmat[...], ybuf[ycorner : ycorner + 4 * dr, :])
    add_layers(mid, lambda p: ring_side(p) + ybuf[ymsg + p * mrows + ov : ymsg + p * mrows + ov + hrows[p], :].astype(F32))
    wait_am()
    gathered = arrived()
    cout = dot(sext[...], gathered).astype(BF16)
    sub[1, own:, :] = (edge2[: 4 * ov, :] + dot(am_r[...], gathered)).astype(BF16)
    mid[...] += dot(abextb[...], cout)
    sub[1, :own, :] = mid[...].astype(BF16)

    arrived = start_gather(1, dot(basis_ref[...], sub[1]))
    sol_ref[...] = xs[...] + dot(bextb[...], cout)
    pm = dot(inv_v[own:, :], sub[1]).astype(BF16)
    made = dot(gmat[: 4 * halo + 4 * dr2, :yedge], pm)
    ring[...] = made[: 4 * halo]
    dsend2[...] = made[4 * halo :].astype(BF16)
    wait_corners = trade(
        lambda p: [remote(dsend2.at[pl.ds(p * dr2, dr2)], drecv2.at[pl.ds(p * dr2, dr2)], dsem_s.at[1, p], dsem_r.at[1, p], cdev[p])],
        has_c, has_cd,
    )
    xs[...] = dot(inv_v[:own, :], sub[1])
    for p in range(4):
        msg2_s[p, :ov, :] = pm[(p ^ 1) * ov : ((p ^ 1) + 1) * ov]
        msg2_s[p, ov : ov + hrows[p], :] = layer_rows(xs, p).astype(BF16)
    wait_back = trade(
        lambda p: [remote(msg2_s.at[p], msg2_r.at[p], nsem_s.at[2, p], nsem_r.at[2, p], up[p])],
        has_up, has_down,
    )
    wait_back()
    backs = jnp.concatenate([msg2_r[p, :ov, :] for p in range(4)], axis=0)
    xs[...] += dot(sel[...], backs)
    sol_ref[...] += xs[...]
    operate(xs, fin_ref, mid)
    wait_corners()
    ring[...] += dot(pmat2[...], drecv2[...])
    add_layers(fin_ref, lambda p: ring_side(p) + msg2_r[p, ov : ov + hrows[p], :].astype(F32))
    gathered = arrived()
    cout = dot(sext[...], gathered).astype(BF16)
    fin_ref[...] += dot(abextb[...], cout)
    sol_ref[...] += dot(bextb[...], cout)
    for end in finish:
        end()


def emit(sol_ref, fin_ref, sol_hbm, fin_hbm, sem):
    pairs = ((sol_ref, sol_hbm), (fin_ref, fin_hbm))
    copies = [pltpu.make_async_copy(x, y, sem.at[k]) for k, (x, y) in enumerate(pairs)]
    for c in copies:
        c.start()
    for c in copies:
        c.wait()


def solution(mesh):
    gx, gy = mesh.shape["gx"], mesh.shape["gy"]

    def per_device(residual, stiffness, local_inverse, coarse_basis, coarse_rows, send_rows, partition_map):
        comps, cx, cy, nv = residual.shape
        own, layer = comps * cx * cy, cx * cy
        m = local_inverse.shape[-1]
        ov = send_rows.shape[-1]
        kw, kd = coarse_rows.shape[-2:]
        halo = comps * max(cx, cy)
        def whole(count, of):
            return -(-count // of) * of

        lanes = whole(9 * kw, 128)
        dr, dr2 = whole(15 * comps, 16), whole(4 * comps, 16)
        crows = whole(6 * comps, 16)
        mrows = ov + 3 * halo + crows
        ny = whole(4 * (ov + halo + mrows + dr), 128)
        grows = 4 * (halo + crows + dr)
        vm = pl.BlockSpec(memory_space=pltpu.VMEM)
        anywhere = pl.BlockSpec(memory_space=pl.ANY)
        dma = pltpu.SemaphoreType.DMA
        out = pl.pallas_call(
            functools.partial(kernel, gx, gy, (comps, cx, cy, nv)),
            out_shape=[pltpu.VMEM((own, nv), F32)] * 2,
            in_specs=[anywhere] * 7,
            out_specs=[vm, vm],
            scratch_shapes=[
                pltpu.VMEM((own, nv), F32),
                pltpu.VMEM((cx, cy), F32),
                pltpu.VMEM((m, m), BF16),
                pltpu.VMEM((kw, m), BF16),
                pltpu.VMEM((kw, kd), BF16),
                pltpu.VMEM((4, ov), jnp.int32),
                pltpu.VMEM((1, gx * gy), jnp.int32),
                pltpu.VMEM((2, m, nv), BF16),
                pltpu.VMEM((own, 4 * ov), BF16),
                pltpu.VMEM((4, ov, 2 * halo), BF16),
                pltpu.VMEM((2, 4 * ov, nv), BF16),
                pltpu.VMEM((ny, nv), BF16),
                pltpu.VMEM((8, ny), F32),
                pltpu.VMEM((grows, 128), F32),
                pltpu.VMEM((4 * ov, 128), F32),
                pltpu.VMEM((4 * ov, 128), F32),
                pltpu.VMEM((grows, 4 * ov + 4 * halo), BF16),
                pltpu.VMEM((8 * ov, ny), BF16),
                pltpu.VMEM((4 * halo, 4 * dr), BF16),
                pltpu.VMEM((4 * halo, 4 * dr2), BF16),
                pltpu.VMEM((4 * halo, nv), F32),
                pltpu.VMEM((4, mrows, nv), BF16),
                pltpu.VMEM((4, dr, nv), BF16),
                pltpu.VMEM((4, ov + halo, nv), BF16),
                pltpu.VMEM((4, ov + halo, nv), BF16),
                pltpu.VMEM((4 * dr2, nv), BF16),
                pltpu.VMEM((4 * dr2, nv), BF16),
                pltpu.VMEM((4, 8, 4 * ov), F32),
                pltpu.VMEM((4, 8, 4 * ov), F32),
                pltpu.VMEM((4, 8, 4 * ov), F32),
                pltpu.VMEM((4, 8, 4 * ov), F32),
                pltpu.VMEM((2, gx * gy, kw, nv), BF16),
                pltpu.VMEM((9, kw, m), BF16),
                pltpu.VMEM((9, kw, kd), BF16),
                pltpu.VMEM((lanes, kd), BF16),
                pltpu.VMEM((m, lanes), F32),
                pltpu.VMEM((own, lanes), F32),
                pltpu.VMEM((own, lanes), F32),
                pltpu.VMEM((own, lanes), BF16),
                pltpu.VMEM((own, lanes), BF16),
                pltpu.VMEM((4 * ov, kd), BF16),
                pltpu.VMEM((4 * ov, kd), BF16),
                pltpu.VMEM((max(4 * ov, 4 * halo), nv), F32),
                pltpu.VMEM((layer, nv), F32),
                pltpu.VMEM((layer, nv), F32),
                pltpu.VMEM((layer, nv), F32),
                pltpu.VMEM((own, nv), F32),
                pltpu.VMEM((own, nv), F32),
                dma((7,)),
                dma((3, 4)),
                dma((3, 4)),
                dma((2, 4)),
                dma((2, 4)),
                dma((5, 4)),
                dma((5, 4)),
                dma((2, 4)),
                dma((2, 4)),
                dma((2,)),
                dma((2,)),
            ],
            compiler_params=pltpu.CompilerParams(collective_id=0, has_side_effects=True),
        )(
            residual.reshape(own, nv),
            stiffness,
            local_inverse[0, 0],
            coarse_basis[0, 0],
            coarse_rows[0, 0],
            send_rows[0, 0],
            partition_map.reshape(1, -1),
        )
        out = pl.pallas_call(
            emit,
            out_shape=[jax.ShapeDtypeStruct((own, nv), F32)] * 2,
            in_specs=[vm, vm],
            out_specs=[anywhere, anywhere],
            scratch_shapes=[dma((2,))],
        )(*[pltpu.with_memory_space_constraint(o, pltpu.VMEM) for o in out])
        return tuple(o.reshape(residual.shape) for o in out)

    placed = (
        P(None, "gx", "gy", None),
        P("gx", "gy"),
        P("gx", "gy", None, None),
        P("gx", "gy", None, None),
        P("gx", "gy", None, None),
        P("gx", "gy", None, None),
        P(),
    )
    return jax.shard_map(
        per_device,
        mesh=mesh,
        in_specs=placed,
        out_specs=(P(None, "gx", "gy", None), P(None, "gx", "gy", None)),
        check_vma=False,
    )
```

time: 28.4 us -> 27.3 us (0.961)
  local copies, waits for them, and re-layouts: 1.49 us -> 0 us
  Pallas kernels: 26.1 us -> 26.4 us
    unnamed x2 -> x0, local copies, waits for them, and re-layouts: 1.49 us -> none
    pallas_call x0 -> x1, Pallas kernels: none -> 0.89 us  [per_device(): pl.pallas_call(emit, out_shape=[jax.ShapeDtypeStruct((own, nv), F32)] * 2...]
    pallas_call x1, Pallas kernels: 26.1 us -> 25.5 us  [per_device(): pl.pallas_call(functools.partial(kernel, gx, gy, (comps, cx, cy, nv)), ou...]
where the time goes in v2:
time: 27.3 us; the launch traced here: 27.1 us
  Pallas kernels  26.4 us (97%)
  between operations  0.64 us (2%)
    pallas_call x1, Pallas kernels, per_device(): pl.pallas_call(functools.partial(kernel, gx, gy, (comps, cx, cy, nv)), ou...  25.5 us
    pallas_call x1, Pallas kernels, per_device(): pl.pallas_call(emit, out_shape=[jax.ShapeDtypeStruct((own, nv), F32)] * 2...  0.89 us

profile of v2, /device:TPU:0, one launch (start us, length us, event | category | flops | bytes accessed | tf_op | source)
XLA Modules:
  0.0 27.1 jit_solution(11840484055268190283)
XLA Ops:
  0.6 25.5 %shard_map.86 = (f32[768,128]{1,0:T(8,128)S(1)}, f32[768,128]{1,0:T(8,128)S(1)}) custom-call(f32[768,128]{1,0:T(8,128)} %bitcast.9, f32[16,16]{1,0:T(8,128)} %stiff_hbm.1, bf16[1024,1024]{1,0:T(8,128)(2,1)} %bitcast.8, bf16[8,1024]{1,0:T(8,128)(2,1)} %bitcast.10, bf16[8,256]{1,0:T(8,128)(2,1)} %bitcast.11, s32[4,64]{1,0:T(4,128)} %bitcast.12, s32[1,32]{1,0:T(1,128)} %bitcast.13), custom_call_target="tpu_custom_call" | custom-call | tf_op jit(solution)/shard_map/pallas_call | solution.py:581
  26.2 0.9 %shard_map.87 = (f32[768,128]{1,0:T(8,128)}, f32[768,128]{1,0:T(8,128)}) custom-call(f32[768,128]{1,0:T(8,128)S(1)} %get-tuple-element.6.sol_ref, f32[768,128]{1,0:T(8,128)S(1)} %get-tuple-element.7.fin_ref), custom_call_target="tpu_custom_call" | custom-call | tf_op jit(solution)/shard_map/pallas_call | solution.py:657

commit v3 on v2

--- a/solution.py
+++ b/solution.py
@@ -17,6 +17,11 @@
     return jnp.dot(x, y, preferred_element_type=F32, **kw)
 
 
+def split(x, y):
+    cut = x.shape[0] // 32 * 16
+    return jnp.concatenate([dot(x[:cut, :], y), dot(x[cut:, :], y)], axis=0)
+
+
 def tdot(x, y):
     return lax.dot_general(x, y, (((0,), (0,)), ((), ())), preferred_element_type=F32)
 
@@ -34,10 +39,11 @@
     res_hbm, stiff_hbm, inv_hbm, basis_hbm, crows_hbm, lists_hbm, pmap_hbm,
     sol_ref, fin_ref,
     res_v, stiff_ref, inv_v, basis_ref, crows_ref, lists_ref, pmap_ref, sub, sel, near, outs,
-    ybuf, ycode, rowc, qb, sb, gmat, mmat, pmat, pmat2, ring, msg_s, dsend, msg2_s, msg2_r, dsend2, drecv2,
+    ybuf, ycode, lines, rowc, qb, sb, gmat, gstat, cown, cmarg, mc, inve, pmv, ring, msg_s, dsend,
+    msg2_s, msg2_r, dsend2, drecv2,
     qs, qr, ts, tr, allbuf, ball, sall, sext, bt, bextf, abf, bextb, abextb, am_s, am_r, edge2,
     diag, m_lo, m_hi, xs, mid,
-    lsem, nsem_s, nsem_r, dsem_s, dsem_r, csem_s, csem_r, rsem_s, rsem_r, gs, gr,
+    lsem, ready, nsem_s, nsem_r, dsem_s, dsem_r, csem_s, csem_r, rsem_s, rsem_r, gs, gr,
 ):
     comps, cx, cy, nv = dims
     halo = comps * max(cx, cy)
@@ -51,9 +57,8 @@
     crows = mrows - ov - 3 * halo
     dr, dr2 = dsend.shape[1], dsend2.shape[0] // 4
     yedge = 4 * ov
-    ymsg = yedge + 4 * halo
-    ycorner = ymsg + 4 * mrows
-    ny = ybuf.shape[0]
+    ycorner = 4 * mrows
+    gpm = 4 * (dr + crows)
     nine = ball.shape[0]
     lanes = bextf.shape[1]
     a = lax.axis_index("gx")
@@ -86,10 +91,14 @@
         to_a = [lax.rem(a + i, gx) for i in range(gx)]
         to_b = [lax.rem(b + j, gy) for j in range(gy)]
 
-    def each_other(act):
+    half = len(others) // 2
+
+    def each_other(act, chosen=None):
         if n <= 64:
-            for i, j in others:
+            for i, j in others if chosen is None else (others[:half], others[half:])[chosen]:
                 act((to_a[i], to_b[j]))
+            return
+        if chosen == 1:
             return
 
         def row(i, _):
@@ -102,7 +111,17 @@
         lax.fori_loop(jnp.int32(0), jnp.int32(gx), row, 0)
 
     barrier = pltpu.get_barrier_semaphore()
-    each_other(lambda dev: pl.semaphore_signal(barrier, inc=1, device_id=dev, device_id_type=MESH))
+
+    def peers(size):
+        return sorted(range(1, size), key=lambda o: min(o, size - o))
+
+    def signal(sem, dev):
+        pl.semaphore_signal(sem, inc=1, device_id=dev, device_id_type=MESH)
+
+    for o in peers(gy):
+        signal(barrier, (a, lax.rem(b + o, gy)))
+    for o in peers(gx):
+        signal(barrier, (lax.rem(a + o, gx), b))
 
     up = [(a + 1, b), (a - 1, b), (a, b + 1), (a, b - 1)]
     has_up = [a < gx - 1, a > 0, b < gy - 1, b > 0]
@@ -179,7 +198,7 @@
             outs[t, p * ov : (p + 1) * ov, :] = dot(near[p, :, : 2 * hrows[p]], rows).astype(BF16)
 
     gather(0, res_v)
-    pl.semaphore_wait(barrier, n - 1)
+    pl.semaphore_wait(barrier, gx + gy - 2)
 
     def start_margins(t):
         return trade(
@@ -193,6 +212,8 @@
 
     wait_margins = start_margins(0)
     has_cd = [has_c[p ^ 1] for p in range(4)]
+    for o in peers(gy):
+        signal(ready, (a, lax.rem(b + o, gy)))
     wait_raw = trade(
         lambda p: [
             remote(basis_hbm, ball.at[1 + p], csem_s.at[1, p], csem_r.at[1, p], up[p]),
@@ -200,20 +221,13 @@
         ],
         has_up, has_down,
     )
-    wait_raw_c = trade(
-        lambda p: [
-            remote(basis_hbm, ball.at[5 + p], rsem_s.at[0, p], rsem_r.at[0, p], cdev[p]),
-            remote(crows_hbm, sall.at[5 + p], rsem_s.at[1, p], rsem_r.at[1, p], cdev[p]),
-        ],
-        has_c, has_cd,
-    )
     sub[0, :own, :] = res_v[...].astype(BF16)
 
     for p in range(4):
         @pl.when(jnp.logical_not(has_down[p]))
         def _(p=p):
             sub[0, own + p * ov : own + (p + 1) * ov, :] = jnp.zeros((ov, nv), BF16)
-            ybuf[ymsg + p * mrows : ymsg + (p + 1) * mrows, :] = jnp.zeros((mrows, nv), BF16)
+            ybuf[p * mrows : (p + 1) * mrows, :] = jnp.zeros((mrows, nv), BF16)
             msg2_r[p] = jnp.zeros(msg2_r.shape[1:], BF16)
             qr[p] = jnp.zeros(qr.shape[1:], F32)
             tr[p] = jnp.zeros(tr.shape[1:], F32)
@@ -227,9 +241,6 @@
             drecv2[p * dr2 : (p + 1) * dr2, :] = jnp.zeros((dr2, nv), BF16)
             ball[5 + p] = jnp.zeros(ball.shape[1:], BF16)
             sall[5 + p] = jnp.zeros(sall.shape[1:], BF16)
-
-    if ny > ycorner + 4 * dr:
-        ybuf[ycorner + 4 * dr :, :] = jnp.zeros((ny - ycorner - 4 * dr, nv), BF16)
 
     load_stiff.wait()
     r1 = fiota((layer, cy), 0)
@@ -251,6 +262,15 @@
         ts[p] = jnp.where(jnp.broadcast_to(block, (8, 4 * ov)) == p, at_cells, 0.0)
     wait_t = trade(
         lambda p: [remote(ts.at[p], tr.at[p], csem_s.at[3, p], csem_r.at[3, p], up[p])], has_up, has_down
+    )
+
+    pl.semaphore_wait(ready, gy - 1)
+    wait_raw_c = trade(
+        lambda p: [
+            remote(basis_hbm, ball.at[5 + p], rsem_s.at[0, p], rsem_r.at[0, p], cdev[p]),
+            remote(crows_hbm, sall.at[5 + p], rsem_s.at[1, p], rsem_r.at[1, p], cdev[p]),
+        ],
+        has_c, has_cd,
     )
 
     def edge_cells(w, p, depth, outside):
@@ -302,30 +322,35 @@
     def row_of(count):
         return fiota((1, count), 1)
 
-    tail = []
+    def deduped(cell, p):
+        c, i, j, real = cell
+        return (c, i, j, real if p < 2 else jnp.logical_and(real, jnp.logical_and(i > 0.0, i < cx - 1.0)))
+
+    back_code = [code(lc, li, lj)[p : p + 1] for p in range(4)]
+    edge_code = [coded(edge_cells(row_of(halo), p, 0, False)) for p in range(4)]
+    deep_code = [[coded(edge_cells(row_of(halo), p, d, True)) for d in range(3)] for p in range(4)]
+    beside_code = [coded(beside_cells(row_of(crows), p), -sides[p][0], -sides[p][1]) for p in range(4)]
+    corner_code = [coded(corner_cells(row_of(dr), *corner[m]), *corner[m]) for m in range(4)]
+    short_code = [coded(corner_cells(row_of(dr2), *corner[m]), *corner[m]) for m in range(4)]
+    ycode[0:1, yedge:] = jnp.concatenate(
+        [coded(deduped(edge_cells(row_of(halo), p, 0, False), p)) for p in range(4)], axis=1
+    )
+    line = []
     for p in range(4):
-        c, i, j, real = edge_cells(row_of(halo), p, 0, False)
-        if p >= 2:
-            real = jnp.logical_and(real, jnp.logical_and(i > 0.0, i < cx - 1.0))
-        tail.append(coded((c, i, j, real)))
-    for p in range(4):
-        ux, uy = -sides[p][0], -sides[p][1]
-        tail.append(code(lc, li, lj)[p : p + 1])
-        tail += [coded(edge_cells(row_of(halo), p, d, True)) for d in range(3)]
-        tail.append(coded(beside_cells(row_of(crows), p), ux, uy))
-    for m in range(4):
-        tail.append(coded(corner_cells(row_of(dr), *corner[m]), *corner[m]))
-    if ny > ycorner + 4 * dr:
-        tail.append(jnp.full((1, ny - ycorner - 4 * dr), nowhere, F32))
-    ycode[0:1, yedge:] = jnp.concatenate(tail, axis=1)
+        line += [back_code[p]] + deep_code[p] + [beside_code[p]]
+    line = jnp.concatenate(line + corner_code, axis=1)
+    lines[...] = jnp.full(lines.shape, nowhere, F32)
+    lines[0:1, : line.shape[1]] = line
+    line = jnp.concatenate(back_code + [deep_code[p][0] for p in range(4)] + short_code, axis=1)
+    lines[1:2, : line.shape[1]] = line
 
     def column_of(count):
         return fiota((count, 128), 0)
 
-    rlist = [coded(edge_cells(column_of(halo), p, 0, True)) for p in range(4)]
-    rlist += [coded(corner_cells(column_of(dr2), *corner[m])) for m in range(4)]
+    rlist = [coded(corner_cells(column_of(dr2), *corner[m])) for m in range(4)]
     rlist += [coded(beside_cells(column_of(crows), p)) for p in range(4)]
     rlist += [coded(corner_cells(column_of(dr - dr2) + dr2, *corner[m])) for m in range(4)]
+    rlist += [coded(edge_cells(column_of(halo), p, 0, True)) for p in range(4)]
     rowc[...] = jnp.concatenate(rlist, axis=0)
 
     def hits(rows, row):
@@ -335,9 +360,15 @@
             parts.append(jnp.where(rows[:, : piece.shape[1]] == piece, 1.0, 0.0))
         return (jnp.concatenate(parts, axis=1) if len(parts) > 1 else parts[0]).astype(BF16)
 
-    pmat[...] = hits(rowc[: 4 * halo, :], ycode[0:1, ycorner : ycorner + 4 * dr])
-    short = [coded(corner_cells(row_of(dr2), *corner[m]), *corner[m]) for m in range(4)]
-    pmat2[...] = hits(rowc[: 4 * halo, :], jnp.concatenate(short, axis=1))
+    def adjacent(gap):
+        return jnp.where(jnp.logical_or(gap == 1.0, gap == wide_grid), 1.0, 0.0)
+
+    def coefficient(gap, weight):
+        return jnp.where(gap == 0.0, -weight, adjacent(gap)).astype(BF16)
+
+    gmat[...] = jnp.zeros(gmat.shape, BF16)
+    first_rest = 4 * (dr2 + crows)
+    gstat[...] = hits(rowc[first_rest:gpm, :], ycode[0:1, yedge:])
 
     rows = fiota((own, ov), 0)
     for h in range(2):
@@ -378,49 +409,63 @@
     def start_gather(t, cin):
         allbuf[t, slot] = cin.astype(BF16)
         here = allbuf.at[t, slot]
-        each_other(lambda dev: remote(here, here, gs.at[t], gr.at[t], dev).start())
         rest = allbuf.at[t, pl.ds(0, n - 1)]
         gathering = remote(rest, rest, gs.at[t], gr.at[t], (to_a[0], to_b[1]))
         finish.append(gathering.wait_send)
 
+        def go(chosen):
+            each_other(lambda dev: remote(here, here, gs.at[t], gr.at[t], dev).start(), chosen)
+
         def arrived():
             gathering.wait_recv()
             return allbuf[t].astype(F32).reshape(kd, nv).astype(BF16)
 
-        return arrived
+        return go, arrived
 
     load_basis.wait()
     load_inv.wait()
-    part = dot(inv_v[:, :own], sub[0, :own, :])
+    part = split(inv_v.at[:, pl.ds(0, own)], sub[0, :own, :])
     cpart = dot(basis_ref[:, :own], sub[0, :own, :])
     wait_margins()
     edge = sub[0, own:, :]
-    arrived = start_gather(0, cpart + dot(basis_ref[:, own:], edge))
-    ycode[0:1, :yedge] = (qr[0] + qr[1] + qr[2] + qr[3])[0:1]
-    pm = (part[own:] + dot(inv_v[own:, own:], edge)).astype(BF16)
-    ybuf[:yedge, :] = pm
-    xs[...] = part[:own] + dot(inv_v[:own, own:], edge)
-    ybuf[yedge:ymsg, :] = jnp.concatenate([layer_rows(xs, p) for p in range(4)], axis=0).astype(BF16)
-    gmat[...] = hits(rowc[...], ycode[0:1, :ymsg])
-    made = dot(gmat[...], ybuf[:ymsg, :])
-    ring[...] = made[: 4 * halo]
-    made = made[4 * halo :].astype(BF16)
-    late = 4 * dr2 + 4 * crows
+    go, arrived = start_gather(0, cpart + dot(basis_ref[:, own:], edge))
+    go(0)
+    q = (qr[0] + qr[1] + qr[2] + qr[3])[0:1]
+    ycode[0:1, :yedge] = q
+    tiles = (slice(0, 2 * ov), slice(2 * ov, 4 * ov))
+    for tile in tiles:
+        gmat[: 4 * dr2, tile] = hits(rowc[: 4 * dr2, :], q[:, tile])
+        gmat[first_rest:gpm, tile] = hits(rowc[first_rest:gpm, :], q[:, tile])
+    for h in range(2):
+        at = slice(4 * dr2 + 2 * h * crows, 4 * dr2 + 2 * (h + 1) * crows)
+        gmat[at, tiles[1 - h]] = hits(rowc[at, :], q[:, tiles[1 - h]])
+    pmv[...] = part[own:] + dot(inv_v[own:, own:], edge)
+    pm = pmv[...].astype(BF16)
+    xs[...] = part[:own] + split(inv_v.at[pl.ds(0, own), pl.ds(own, 4 * ov)], edge)
+    edges = jnp.concatenate([layer_rows(xs, p) for p in range(4)], axis=0).astype(BF16)
+    made = split(gmat.at[pl.ds(0, gpm), :], pm)
+    made_first = made[:first_rest].astype(BF16)
+    made_rest = (made[first_rest:] + dot(gstat[...], edges)).astype(BF16)
     for p in range(4):
         msg_s[p, :ov, :] = pm[(p ^ 1) * ov : ((p ^ 1) + 1) * ov]
-        for d in range(3):
+        msg_s[p, ov : ov + halo, :] = edges[p * halo : (p + 1) * halo]
+        for d in range(1, 3):
             msg_s[p, ov + d * halo : ov + d * halo + hrows[p], :] = layer_rows(xs, p, d).astype(BF16)
-        msg_s[p, ov + 3 * halo :, :] = made[4 * dr2 + p * crows : 4 * dr2 + (p + 1) * crows]
-        dsend[p, :dr2, :] = made[p * dr2 : (p + 1) * dr2]
-        dsend[p, dr2:, :] = made[late + p * (dr - dr2) : late + (p + 1) * (dr - dr2)]
+        msg_s[p, ov + 3 * halo :, :] = made_first[4 * dr2 + p * crows : 4 * dr2 + (p + 1) * crows]
+        dsend[p, :dr2, :] = made_first[p * dr2 : (p + 1) * dr2]
+        dsend[p, dr2:, :] = made_rest[p * (dr - dr2) : (p + 1) * (dr - dr2)]
     wait_corners = trade(
         lambda p: [remote(dsend.at[p], ybuf.at[pl.ds(ycorner + p * dr, dr)], dsem_s.at[0, p], dsem_r.at[0, p], cdev[p])],
         has_c, has_cd,
     )
     wait_back = trade(
-        lambda p: [remote(msg_s.at[p], ybuf.at[pl.ds(ymsg + p * mrows, mrows)], nsem_s.at[1, p], nsem_r.at[1, p], up[p])],
+        lambda p: [remote(msg_s.at[p], ybuf.at[pl.ds(p * mrows, mrows)], nsem_s.at[1, p], nsem_r.at[1, p], up[p])],
         has_up, has_down,
     )
+    go(1)
+    for h in range(2):
+        at = slice(gpm + 2 * h * halo, gpm + 2 * (h + 1) * halo)
+        gmat[at, tiles[h]] = hits(rowc[at, :], q[:, tiles[h]])
 
     load_pmap.wait()
     load_crows.wait()
@@ -442,12 +487,12 @@
     theirs = jnp.concatenate([of(1.0 + p, margin(p ^ 1)) for p in range(4)], axis=0).astype(BF16)
     bextf[...] = of(0.0, bt[:own, :]) + dot(sel[...], theirs)
     around_b = jnp.concatenate([of(1.0 + p, layer_rows(bt, p)) for p in range(4)], axis=0)
-    around_b += dot(gmat[: 4 * halo, :yedge], of(0.0, bt[own:, :]).astype(BF16))
+    around_b += dot(gmat[gpm:, :], of(0.0, bt[own:, :]).astype(BF16))
     for m, (sx, sy) in enumerate(corner):
         ky, py = (0 if sx < 0 else 1), (3 if sy < 0 else 2)
         kx, px = (2 if sy < 0 else 3), (1 if sx < 0 else 0)
-        lines = [qr[py, 1:2, ky * ov : (ky + 1) * ov], qr[px, 1:2, kx * ov : (kx + 1) * ov]]
-        oh = hits(rowc[: 4 * halo, :], jnp.concatenate(lines, axis=1))
+        pair = [qr[py, 1:2, ky * ov : (ky + 1) * ov], qr[px, 1:2, kx * ov : (kx + 1) * ov]]
+        oh = hits(rowc[gpm:, :], jnp.concatenate(pair, axis=1))
         around_b += dot(oh, of(5.0 + m, jnp.concatenate([margin(ky), margin(kx)], axis=0)).astype(BF16))
     edge2[: 4 * halo, :] = around_b
     operate(bextf, abf, None)
@@ -486,63 +531,105 @@
     qb[...] = as_column(ycode[0:1, :yedge])
     wait_t()
     sb[...] = as_column((tr[0] + tr[1] + tr[2] + tr[3])[0:1])
-
-    def relate(c, _):
-        at = pl.ds(pl.multiple_of(c * 128, 128), 128)
-        gap = jnp.abs(ycode[0:1, at] - qb[...])
-        mmat[: 4 * ov, at] = jnp.where(gap == 0.0, 1.0, 0.0).astype(BF16)
-        mmat[4 * ov :, at] = jnp.where(jnp.logical_or(gap == 1.0, gap == wide_grid), 1.0, 0.0).astype(BF16)
+    pm = pmv[...].astype(BF16)
+    for h in range(0, cmarg.shape[1], 128):
+        gap = jnp.abs(lines[0:1, h : h + 128] - qb[...])
+        cmarg[:, h : h + 128] = coefficient(gap, sb[...])
+    for p in range(4):
+        at = slice(p * ov, (p + 1) * ov)
+        line = jnp.concatenate([ycode[0:1, at], edge_code[p ^ 1]], axis=1)
+        mc[p] = adjacent(jnp.abs(line - qb[at, : ov + halo])).astype(BF16)
+        near_edge = jnp.concatenate([pm[at], msg_s[p ^ 1, ov : ov + halo, :]], axis=0)
+        known = sub[0, own + p * ov : own + (p + 1) * ov, :].astype(F32)
+        edge2[at, :] = known + dot(mc[p], near_edge) - sb[at, :] * pmv[at, :]
+
+    rc = fiota((layer, 128), 0)
+    ri = fdiv(rc, cy)
+    here_code = code(0.0, ri, rc - ri * cy)
+
+    def fill_own(c, _):
+        at = pl.ds(pl.multiple_of(c * layer, layer), layer)
+        shift = c.astype(F32) * (wide_grid * wide_grid)
+        for h in range(0, cown.shape[1], 128):
+            gap = jnp.abs(here_code + shift - lines[1:2, h : h + 128])
+            cown[at, h : h + 128] = coefficient(gap, diag[:, :128])
         return 0
 
-    lax.fori_loop(jnp.int32(0), jnp.int32(ny // 128), relate, 0)
-
-    wait_back()
-    wait_corners()
-    seen = dot(mmat[...], ybuf[...])
-    edge2m = sub[0, own:, :].astype(F32) + seen[4 * ov :] - sb[...] * seen[: 4 * ov]
-    edge2[: 4 * ov, :] = edge2m
-    backs = jnp.concatenate([ybuf[ymsg + p * mrows : ymsg + p * mrows + ov, :] for p in range(4)], axis=0)
-    xs[...] += dot(sel[...], backs)
+    lax.fori_loop(jnp.int32(0), jnp.int32(comps), fill_own, 0)
+
+    r = fiota((2 * comps * cx, own), 0)
+    lower = jnp.where(r >= comps * cx, 1.0, 0.0)
+    wanted_row = (r - lower * (comps * cx)) * cy + (cy - 1) * (1.0 - lower)
+    pick = jnp.where(fiota((2 * comps * cx, own), 1) == wanted_row, 1.0, 0.0).astype(BF16)
+    inve[...] = dot(pick, inv_v[:own, :]).astype(BF16)
+
     operate(xs, mid, res_v)
-    ring[...] += dot(pmat[...], ybuf[ycorner : ycorner + 4 * dr, :])
-    add_layers(mid, lambda p: ring_side(p) + ybuf[ymsg + p * mrows + ov : ymsg + p * mrows + ov + hrows[p], :].astype(F32))
+    ring[...] = dot(gmat[gpm:, :], pm)
+    add_layers(mid, ring_side)
+
     wait_am()
     gathered = arrived()
     cout = dot(sext[...], gathered).astype(BF16)
-    sub[1, own:, :] = (edge2[: 4 * ov, :] + dot(am_r[...], gathered)).astype(BF16)
+    edge2[: 4 * ov, :] += dot(am_r[...], gathered)
     mid[...] += dot(abextb[...], cout)
-    sub[1, :own, :] = mid[...].astype(BF16)
-
-    arrived = start_gather(1, dot(basis_ref[...], sub[1]))
-    sol_ref[...] = xs[...] + dot(bextb[...], cout)
-    pm = dot(inv_v[own:, :], sub[1]).astype(BF16)
-    made = dot(gmat[: 4 * halo + 4 * dr2, :yedge], pm)
-    ring[...] = made[: 4 * halo]
-    dsend2[...] = made[4 * halo :].astype(BF16)
+
+    wait_back()
+    wait_corners()
+
+    def piece(p, at, count):
+        return ybuf[p * mrows + at : p * mrows + at + count, :]
+
+    pieces = 4 * (mrows + dr)
+    sub[1, own:, :] = (edge2[: 4 * ov, :] + dot(cmarg[:, :pieces], ybuf[...])).astype(BF16)
+    backs = jnp.concatenate([piece(p, 0, ov) for p in range(4)], axis=0)
+    rest = [piece(p, ov, halo) for p in range(4)]
+    rest += [ybuf[ycorner + m * dr : ycorner + m * dr + dr2, :] for m in range(4)]
+    sol_ref[...] = split(cown, jnp.concatenate([backs] + rest, axis=0))
+    value = mid[...] + sol_ref[...]
+    mid[...] = value
+    sub[1, :own, :] = value.astype(BF16)
+
+    go, arrived = start_gather(1, dot(basis_ref[...], sub[1]))
+    go(0)
+    lhs = [inv_v[own:, :]]
+    lhs += [inv_v[c * layer + layer - cy : (c + 1) * layer, :] for c in range(comps)]
+    lhs += [inv_v[c * layer : c * layer + cy, :] for c in range(comps)]
+    made = split(jnp.concatenate(lhs + [inve[...]], axis=0), sub[1])
+    pm = made[: 4 * ov].astype(BF16)
+    at = 4 * ov
+    for p in range(4):
+        msg2_s[p, :ov, :] = pm[(p ^ 1) * ov : ((p ^ 1) + 1) * ov]
+        msg2_s[p, ov : ov + hrows[p], :] = made[at : at + hrows[p]].astype(BF16)
+        at += hrows[p]
+    dsend2[...] = dot(gmat[: 4 * dr2, :], pm).astype(BF16)
     wait_corners = trade(
         lambda p: [remote(dsend2.at[pl.ds(p * dr2, dr2)], drecv2.at[pl.ds(p * dr2, dr2)], dsem_s.at[1, p], dsem_r.at[1, p], cdev[p])],
         has_c, has_cd,
     )
-    xs[...] = dot(inv_v[:own, :], sub[1])
-    for p in range(4):
-        msg2_s[p, :ov, :] = pm[(p ^ 1) * ov : ((p ^ 1) + 1) * ov]
-        msg2_s[p, ov : ov + hrows[p], :] = layer_rows(xs, p).astype(BF16)
     wait_back = trade(
         lambda p: [remote(msg2_s.at[p], msg2_r.at[p], nsem_s.at[2, p], nsem_r.at[2, p], up[p])],
         has_up, has_down,
     )
-    wait_back()
-    backs = jnp.concatenate([msg2_r[p, :ov, :] for p in range(4)], axis=0)
-    xs[...] += dot(sel[...], backs)
+    go(1)
+    sol_ref[...] = xs[...] + dot(bextb[...], cout)
+    sol_ref[...] += dot(sel[...], backs)
+    xs[...] = split(inv_v.at[pl.ds(0, own), :], sub[1])
     sol_ref[...] += xs[...]
     operate(xs, fin_ref, mid)
+    ring[...] = dot(gmat[gpm:, :], pm)
+    add_layers(fin_ref, ring_side)
+    wait_back()
     wait_corners()
-    ring[...] += dot(pmat2[...], drecv2[...])
-    add_layers(fin_ref, lambda p: ring_side(p) + msg2_r[p, ov : ov + hrows[p], :].astype(F32))
+    backs = jnp.concatenate([msg2_r[p, :ov, :] for p in range(4)], axis=0)
+    rest = jnp.concatenate([msg2_r[p, ov:, :] for p in range(4)] + [drecv2[...]], axis=0)
+    both = jnp.concatenate([backs, rest], axis=0)
+    xs[...] = split(cown, both)
+    fin_ref[...] += xs[...]
+    sol_ref[...] += split(sel, backs)
     gathered = arrived()
     cout = dot(sext[...], gathered).astype(BF16)
-    fin_ref[...] += dot(abextb[...], cout)
-    sol_ref[...] += dot(bextb[...], cout)
+    fin_ref[...] += split(abextb, cout)
+    sol_ref[...] += split(bextb, cout)
     for end in finish:
         end()
 
@@ -573,7 +660,7 @@
         dr, dr2 = whole(15 * comps, 16), whole(4 * comps, 16)
         crows = whole(6 * comps, 16)
         mrows = ov + 3 * halo + crows
-        ny = whole(4 * (ov + halo + mrows + dr), 128)
+        width = whole(4 * (mrows + dr), 128)
         grows = 4 * (halo + crows + dr)
         vm = pl.BlockSpec(memory_space=pltpu.VMEM)
         anywhere = pl.BlockSpec(memory_space=pl.ANY)
@@ -595,15 +682,19 @@
                 pltpu.VMEM((own, 4 * ov), BF16),
                 pltpu.VMEM((4, ov, 2 * halo), BF16),
                 pltpu.VMEM((2, 4 * ov, nv), BF16),
-                pltpu.VMEM((ny, nv), BF16),
-                pltpu.VMEM((8, ny), F32),
+                pltpu.VMEM((4 * (mrows + dr), nv), BF16),
+                pltpu.VMEM((8, 4 * ov + 4 * halo), F32),
+                pltpu.VMEM((8, width), F32),
                 pltpu.VMEM((grows, 128), F32),
                 pltpu.VMEM((4 * ov, 128), F32),
                 pltpu.VMEM((4 * ov, 128), F32),
-                pltpu.VMEM((grows, 4 * ov + 4 * halo), BF16),
-                pltpu.VMEM((8 * ov, ny), BF16),
-                pltpu.VMEM((4 * halo, 4 * dr), BF16),
-                pltpu.VMEM((4 * halo, 4 * dr2), BF16),
+                pltpu.VMEM((grows, 4 * ov), BF16),
+                pltpu.VMEM((4 * (dr - dr2), 4 * halo), BF16),
+                pltpu.VMEM((own, 4 * (ov + halo + dr2)), BF16),
+                pltpu.VMEM((4 * ov, width), BF16),
+                pltpu.VMEM((4, ov, ov + halo), BF16),
+                pltpu.VMEM((2 * comps * cx, m), BF16),
+                pltpu.VMEM((4 * ov, nv), F32),
                 pltpu.VMEM((4 * halo, nv), F32),
                 pltpu.VMEM((4, mrows, nv), BF16),
                 pltpu.VMEM((4, dr, nv), BF16),
@@ -633,6 +724,7 @@
                 pltpu.VMEM((own, nv), F32),
                 pltpu.VMEM((own, nv), F32),
                 dma((7,)),
+                pltpu.SemaphoreType.REGULAR,
                 dma((3, 4)),
                 dma((3, 4)),
                 dma((2, 4)),

time: 27.3 us -> 26.2 us (0.960)
  Pallas kernels: 26.4 us -> 25.3 us
    pallas_call x1, Pallas kernels: 25.5 us -> 24.5 us  [per_device(): pl.pallas_call(functools.partial(kernel, gx, gy, (comps, cx, cy, nv)), ou...]
where the time goes in v3:
time: 26.2 us; the launch traced here: 26 us
  Pallas kernels  25.3 us (97%)
  between operations  0.64 us (2%)
    pallas_call x1, Pallas kernels, per_device(): pl.pallas_call(functools.partial(kernel, gx, gy, (comps, cx, cy, nv)), ou...  24.5 us
    pallas_call x1, Pallas kernels, per_device(): pl.pallas_call(emit, out_shape=[jax.ShapeDtypeStruct((own, nv), F32)] * 2...  0.89 us

profile of v3, /device:TPU:0, one launch (start us, length us, event | category | flops | bytes accessed | tf_op | source)
XLA Modules:
  0.0 26.0 jit_solution(4293811072716731392)
XLA Ops:
  0.6 24.5 %shard_map.86 = (f32[768,128]{1,0:T(8,128)S(1)}, f32[768,128]{1,0:T(8,128)S(1)}) custom-call(f32[768,128]{1,0:T(8,128)} %bitcast.9, f32[16,16]{1,0:T(8,128)} %stiff_hbm.1, bf16[1024,1024]{1,0:T(8,128)(2,1)} %bitcast.8, bf16[8,1024]{1,0:T(8,128)(2,1)} %bitcast.10, bf16[8,256]{1,0:T(8,128)(2,1)} %bitcast.11, s32[4,64]{1,0:T(4,128)} %bitcast.12, s32[1,32]{1,0:T(1,128)} %bitcast.13), custom_call_target="tpu_custom_call" | custom-call | tf_op jit(solution)/shard_map/pallas_call | solution.py:668
  25.1 0.9 %shard_map.87 = (f32[768,128]{1,0:T(8,128)}, f32[768,128]{1,0:T(8,128)}) custom-call(f32[768,128]{1,0:T(8,128)S(1)} %get-tuple-element.6.sol_ref, f32[768,128]{1,0:T(8,128)S(1)} %get-tuple-element.7.fin_ref), custom_call_target="tpu_custom_call" | custom-call | tf_op jit(solution)/shard_map/pallas_call | solution.py:749

commit v4 on v3

--- a/solution.py
+++ b/solution.py
@@ -134,6 +134,9 @@
     ]
     finish = []
 
+    for p in range(4):
+        pl.when(has_c[p])(lambda p=p: signal(barrier, cdev[p]))
+
     def send(copies, conds, wait):
         for p in (2, 3, 0, 1):
             @pl.when(conds[p])
@@ -198,7 +201,8 @@
             outs[t, p * ov : (p + 1) * ov, :] = dot(near[p, :, : 2 * hrows[p]], rows).astype(BF16)
 
     gather(0, res_v)
-    pl.semaphore_wait(barrier, gx + gy - 2)
+    met = gx + gy - 2 + sum(c.astype(jnp.int32) for c in has_c)
+    pl.semaphore_wait(barrier, met)
 
     def start_margins(t):
         return trade(
@@ -214,12 +218,21 @@
     has_cd = [has_c[p ^ 1] for p in range(4)]
     for o in peers(gy):
         signal(ready, (a, lax.rem(b + o, gy)))
+    load_basis.wait()
+    load_crows.wait()
     wait_raw = trade(
         lambda p: [
-            remote(basis_hbm, ball.at[1 + p], csem_s.at[1, p], csem_r.at[1, p], up[p]),
-            remote(crows_hbm, sall.at[1 + p], csem_s.at[2, p], csem_r.at[2, p], up[p]),
+            remote(basis_ref, ball.at[1 + p], csem_s.at[1, p], csem_r.at[1, p], up[p]),
+            remote(crows_ref, sall.at[1 + p], csem_s.at[2, p], csem_r.at[2, p], up[p]),
         ],
         has_up, has_down,
+    )
+    wait_raw_c = trade(
+        lambda p: [
+            remote(basis_ref.at[:, pl.ds(own, 4 * ov)], ball.at[5 + p, :, pl.ds(own, 4 * ov)], rsem_s.at[0, p], rsem_r.at[0, p], cdev[p]),
+            remote(crows_ref, sall.at[5 + p], rsem_s.at[1, p], rsem_r.at[1, p], cdev[p]),
+        ],
+        has_c, has_cd,
     )
     sub[0, :own, :] = res_v[...].astype(BF16)
 
@@ -239,8 +252,11 @@
         def _(p=p):
             ybuf[ycorner + p * dr : ycorner + (p + 1) * dr, :] = jnp.zeros((dr, nv), BF16)
             drecv2[p * dr2 : (p + 1) * dr2, :] = jnp.zeros((dr2, nv), BF16)
-            ball[5 + p] = jnp.zeros(ball.shape[1:], BF16)
+            ball[5 + p, :, own:] = jnp.zeros((kw, 4 * ov), BF16)
             sall[5 + p] = jnp.zeros(sall.shape[1:], BF16)
+
+    for p in range(4):
+        ball[5 + p, :, :own] = jnp.zeros((kw, own), BF16)
 
     load_stiff.wait()
     r1 = fiota((layer, cy), 0)
@@ -262,15 +278,6 @@
         ts[p] = jnp.where(jnp.broadcast_to(block, (8, 4 * ov)) == p, at_cells, 0.0)
     wait_t = trade(
         lambda p: [remote(ts.at[p], tr.at[p], csem_s.at[3, p], csem_r.at[3, p], up[p])], has_up, has_down
-    )
-
-    pl.semaphore_wait(ready, gy - 1)
-    wait_raw_c = trade(
-        lambda p: [
-            remote(basis_hbm, ball.at[5 + p], rsem_s.at[0, p], rsem_r.at[0, p], cdev[p]),
-            remote(crows_hbm, sall.at[5 + p], rsem_s.at[1, p], rsem_r.at[1, p], cdev[p]),
-        ],
-        has_c, has_cd,
     )
 
     def edge_cells(w, p, depth, outside):
@@ -422,13 +429,13 @@
 
         return go, arrived
 
-    load_basis.wait()
     load_inv.wait()
     part = split(inv_v.at[:, pl.ds(0, own)], sub[0, :own, :])
     cpart = dot(basis_ref[:, :own], sub[0, :own, :])
     wait_margins()
     edge = sub[0, own:, :]
     go, arrived = start_gather(0, cpart + dot(basis_ref[:, own:], edge))
+    pl.semaphore_wait(ready, gy - 1)
     go(0)
     q = (qr[0] + qr[1] + qr[2] + qr[3])[0:1]
     ycode[0:1, :yedge] = q
@@ -468,7 +475,6 @@
         gmat[at, tiles[h]] = hits(rowc[at, :], q[:, tiles[h]])
 
     load_pmap.wait()
-    load_crows.wait()
     wait_raw()
     wait_raw_c()
     ball[0] = basis_ref[...]

time: 26.2 us -> 25.6 us (0.977)
  Pallas kernels: 25.3 us -> 24.8 us
    pallas_call x1, Pallas kernels: 24.5 us -> 23.9 us  [per_device(): pl.pallas_call(functools.partial(kernel, gx, gy, (comps, cx, cy, nv)), ou...]
where the time goes in v4:
time: 25.6 us; the launch traced here: 25.4 us
  Pallas kernels  24.8 us (97%)
  between operations  0.64 us (2%)
    pallas_call x1, Pallas kernels, per_device(): pl.pallas_call(functools.partial(kernel, gx, gy, (comps, cx, cy, nv)), ou...  23.9 us
    pallas_call x1, Pallas kernels, per_device(): pl.pallas_call(emit, out_shape=[jax.ShapeDtypeStruct((own, nv), F32)] * 2...  0.89 us

profile of v4, /device:TPU:0, one launch (start us, length us, event | category | flops | bytes accessed | tf_op | source)
XLA Modules:
  0.0 25.4 jit_solution(6767952971318315780)
XLA Ops:
  0.6 23.9 %shard_map.86 = (f32[768,128]{1,0:T(8,128)S(1)}, f32[768,128]{1,0:T(8,128)S(1)}) custom-call(f32[768,128]{1,0:T(8,128)} %bitcast.9, f32[16,16]{1,0:T(8,128)} %stiff_hbm.1, bf16[1024,1024]{1,0:T(8,128)(2,1)} %bitcast.8, bf16[8,1024]{1,0:T(8,128)(2,1)} %bitcast.10, bf16[8,256]{1,0:T(8,128)(2,1)} %bitcast.11, s32[4,64]{1,0:T(4,128)} %bitcast.12, s32[1,32]{1,0:T(1,128)} %bitcast.13), custom_call_target="tpu_custom_call" | custom-call | tf_op jit(solution)/shard_map/pallas_call | solution.py:674
  24.5 0.9 %shard_map.87 = (f32[768,128]{1,0:T(8,128)}, f32[768,128]{1,0:T(8,128)}) custom-call(f32[768,128]{1,0:T(8,128)S(1)} %get-tuple-element.6.sol_ref, f32[768,128]{1,0:T(8,128)S(1)} %get-tuple-element.7.fin_ref), custom_call_target="tpu_custom_call" | custom-call | tf_op jit(solution)/shard_map/pallas_call | solution.py:755

commit v5 on v4

--- a/solution.py
+++ b/solution.py
@@ -41,7 +41,7 @@
     res_v, stiff_ref, inv_v, basis_ref, crows_ref, lists_ref, pmap_ref, sub, sel, near, outs,
     ybuf, ycode, lines, rowc, qb, sb, gmat, gstat, cown, cmarg, mc, inve, pmv, ring, msg_s, dsend,
     msg2_s, msg2_r, dsend2, drecv2,
-    qs, qr, ts, tr, allbuf, ball, sall, sext, bt, bextf, abf, bextb, abextb, am_s, am_r, edge2,
+    qs, qr, qd_s, qd_r, ts, tr, allbuf, ball, sall, sext, bt, bextf, abf, bextb, abextb, yb, mbb, edge2,
     diag, m_lo, m_hi, xs, mid,
     lsem, ready, nsem_s, nsem_r, dsem_s, dsem_r, csem_s, csem_r, rsem_s, rsem_r, gs, gr,
 ):
@@ -218,6 +218,8 @@
     has_cd = [has_c[p ^ 1] for p in range(4)]
     for o in peers(gy):
         signal(ready, (a, lax.rem(b + o, gy)))
+    for m, (sx, sy) in enumerate(corner):
+        qd_s[m, 0:1, :] = in_line(code(lc, li - sx * cx, lj - sy * cy))
     load_basis.wait()
     load_crows.wait()
     wait_raw = trade(
@@ -229,7 +231,8 @@
     )
     wait_raw_c = trade(
         lambda p: [
-            remote(basis_ref.at[:, pl.ds(own, 4 * ov)], ball.at[5 + p, :, pl.ds(own, 4 * ov)], rsem_s.at[0, p], rsem_r.at[0, p], cdev[p]),
+            remote(basis_ref, ball.at[5 + p], rsem_s.at[0, p], rsem_r.at[0, p], cdev[p]),
+            remote(qd_s.at[p], qd_r.at[p], rsem_s.at[2, p], rsem_r.at[2, p], cdev[p]),
             remote(crows_ref, sall.at[5 + p], rsem_s.at[1, p], rsem_r.at[1, p], cdev[p]),
         ],
         has_c, has_cd,
@@ -244,7 +247,6 @@
             msg2_r[p] = jnp.zeros(msg2_r.shape[1:], BF16)
             qr[p] = jnp.zeros(qr.shape[1:], F32)
             tr[p] = jnp.zeros(tr.shape[1:], F32)
-            am_r[p * ov : (p + 1) * ov, :] = jnp.zeros((ov, kd), BF16)
             ball[1 + p] = jnp.zeros(ball.shape[1:], BF16)
             sall[1 + p] = jnp.zeros(sall.shape[1:], BF16)
 
@@ -252,11 +254,9 @@
         def _(p=p):
             ybuf[ycorner + p * dr : ycorner + (p + 1) * dr, :] = jnp.zeros((dr, nv), BF16)
             drecv2[p * dr2 : (p + 1) * dr2, :] = jnp.zeros((dr2, nv), BF16)
-            ball[5 + p, :, own:] = jnp.zeros((kw, 4 * ov), BF16)
+            ball[5 + p] = jnp.zeros(ball.shape[1:], BF16)
+            qd_r[p] = jnp.zeros(qd_r.shape[1:], F32)
             sall[5 + p] = jnp.zeros(sall.shape[1:], BF16)
-
-    for p in range(4):
-        ball[5 + p, :, :own] = jnp.zeros((kw, own), BF16)
 
     load_stiff.wait()
     r1 = fiota((layer, cy), 0)
@@ -505,7 +505,31 @@
     add_layers(abf, lambda p: edge2[p * halo : p * halo + hrows[p], :])
     bextb[...] = bextf[...].astype(BF16)
     abextb[...] = abf[...].astype(BF16)
-    gather(1, abf)
+
+    for p in range(4):
+        pieces = [of(1.0 + p, margin(p ^ 1))] + [of(1.0 + p, layer_rows(bt, p, d)) for d in range(3)]
+        yb[p * mrows : p * mrows + ov + 3 * halo, :] = jnp.concatenate(pieces, axis=0).astype(BF16)
+        cells = coded(beside_cells(column_of(crows), p), -sides[p][0], -sides[p][1])
+        row = []
+        for u, k in ((-1, 2), (1, 3)) if p < 2 else ((-1, 0), (1, 1)):
+            way = (-sides[p][0], -u) if p < 2 else (-u, -sides[p][1])
+            row.append(qd_r[corner.index(way), 0:1, k * ov : (k + 1) * ov])
+        k = 2 if p < 2 else 0
+        theirs = of(1.0 + p, bt[own + k * ov : own + (k + 2) * ov, :]).astype(BF16)
+        made = dot(hits(cells, jnp.concatenate(row, axis=1)), theirs)
+        yb[p * mrows + ov + 3 * halo : (p + 1) * mrows, :] = made.astype(BF16)
+    for m, (sx, sy) in enumerate(corner):
+        ky, py = (0 if sx < 0 else 1), (3 if sy < 0 else 2)
+        kx, px = (2 if sy < 0 else 3), (1 if sx < 0 else 0)
+        pair = [qr[py, 1:2, ky * ov : (ky + 1) * ov], qr[px, 1:2, kx * ov : (kx + 1) * ov]]
+        cells = coded(corner_cells(column_of(dr), sx, sy), sx, sy)
+        theirs = of(5.0 + m, jnp.concatenate([margin(ky), margin(kx)], axis=0)).astype(BF16)
+        made = dot(hits(cells, jnp.concatenate(pair, axis=1)), theirs)
+        theirs = jnp.concatenate([layer_rows(bt, q) for q in range(4)], axis=0)
+        rest = dot(gstat[m * (dr - dr2) : (m + 1) * (dr - dr2), :], of(5.0 + m, theirs).astype(BF16))
+        at = ycorner + m * dr
+        yb[at : at + dr2, :] = made[:dr2].astype(BF16)
+        yb[at + dr2 : at + dr, :] = (made[dr2:] + rest).astype(BF16)
 
     wide = min(kd, 256)
     pmf = jnp.broadcast_to(pmap_ref[...].astype(F32), (8, n))
@@ -522,15 +546,9 @@
         perm = jnp.where(fiota((kd, wide), 0) == place, 1.0, 0.0).astype(BF16)
         at = pl.ds(pl.multiple_of(c * wide, wide), wide)
         sext[:, at] = dot(stacked_s, perm).astype(BF16)
-        am_s[:, at] = dot(outs[1], sext[:, at]).astype(BF16)
         return 0
 
     lax.fori_loop(jnp.int32(0), jnp.int32(kd // wide), order, 0)
-    wait_am = trade(
-        lambda p: [remote(am_s.at[pl.ds(p * ov, ov)], am_r.at[pl.ds(p * ov, ov)], csem_s.at[4, p], csem_r.at[4, p], up[p])],
-        has_up, has_down,
-    )
-
     def as_column(line):
         return jnp.broadcast_to(jnp.broadcast_to(line, (8, 4 * ov)).T[:, 0:1], (4 * ov, 128))
 
@@ -541,11 +559,16 @@
     for h in range(0, cmarg.shape[1], 128):
         gap = jnp.abs(lines[0:1, h : h + 128] - qb[...])
         cmarg[:, h : h + 128] = coefficient(gap, sb[...])
+    mix = dot(cmarg[:, : 4 * (mrows + dr)], yb[...])
     for p in range(4):
         at = slice(p * ov, (p + 1) * ov)
         line = jnp.concatenate([ycode[0:1, at], edge_code[p ^ 1]], axis=1)
         mc[p] = adjacent(jnp.abs(line - qb[at, : ov + halo])).astype(BF16)
         near_edge = jnp.concatenate([pm[at], msg_s[p ^ 1, ov : ov + halo, :]], axis=0)
+        near_b = [of(0.0, margin(p)), of(0.0, layer_rows(bt, p ^ 1))]
+        near_b = jnp.concatenate(near_b, axis=0).astype(BF16)
+        mine = dot(mc[p], near_b) - sb[at, :] * of(0.0, margin(p))
+        mbb[at, :] = (mix[at] + mine).astype(BF16)
         known = sub[0, own + p * ov : own + (p + 1) * ov, :].astype(F32)
         edge2[at, :] = known + dot(mc[p], near_edge) - sb[at, :] * pmv[at, :]
 
@@ -573,10 +596,9 @@
     ring[...] = dot(gmat[gpm:, :], pm)
     add_layers(mid, ring_side)
 
-    wait_am()
     gathered = arrived()
     cout = dot(sext[...], gathered).astype(BF16)
-    edge2[: 4 * ov, :] += dot(am_r[...], gathered)
+    edge2[: 4 * ov, :] += dot(mbb[...], cout)
     mid[...] += dot(abextb[...], cout)
 
     wait_back()
@@ -607,14 +629,14 @@
         msg2_s[p, :ov, :] = pm[(p ^ 1) * ov : ((p ^ 1) + 1) * ov]
         msg2_s[p, ov : ov + hrows[p], :] = made[at : at + hrows[p]].astype(BF16)
         at += hrows[p]
+    wait_back = trade(
+        lambda p: [remote(msg2_s.at[p], msg2_r.at[p], nsem_s.at[2, p], nsem_r.at[2, p], up[p])],
+        has_up, has_down,
+    )
     dsend2[...] = dot(gmat[: 4 * dr2, :], pm).astype(BF16)
     wait_corners = trade(
         lambda p: [remote(dsend2.at[pl.ds(p * dr2, dr2)], drecv2.at[pl.ds(p * dr2, dr2)], dsem_s.at[1, p], dsem_r.at[1, p], cdev[p])],
         has_c, has_cd,
-    )
-    wait_back = trade(
-        lambda p: [remote(msg2_s.at[p], msg2_r.at[p], nsem_s.at[2, p], nsem_r.at[2, p], up[p])],
-        has_up, has_down,
     )
     go(1)
     sol_ref[...] = xs[...] + dot(bextb[...], cout)
@@ -641,8 +663,13 @@
 
 
 def emit(sol_ref, fin_ref, sol_hbm, fin_hbm, sem):
-    pairs = ((sol_ref, sol_hbm), (fin_ref, fin_hbm))
-    copies = [pltpu.make_async_copy(x, y, sem.at[k]) for k, (x, y) in enumerate(pairs)]
+    parts = sem.shape[0] // 2
+    size = sol_ref.shape[0] // parts
+    copies = []
+    for k in range(parts):
+        at = pl.ds(k * size, size)
+        for h, (x, y) in enumerate(((sol_ref, sol_hbm), (fin_ref, fin_hbm))):
+            copies.append(pltpu.make_async_copy(x.at[at], y.at[at], sem.at[2 * k + h]))
     for c in copies:
         c.start()
     for c in copies:
@@ -712,6 +739,8 @@
                 pltpu.VMEM((4, 8, 4 * ov), F32),
                 pltpu.VMEM((4, 8, 4 * ov), F32),
                 pltpu.VMEM((4, 8, 4 * ov), F32),
+                pltpu.VMEM((4, 8, 4 * ov), F32),
+                pltpu.VMEM((4, 8, 4 * ov), F32),
                 pltpu.VMEM((2, gx * gy, kw, nv), BF16),
                 pltpu.VMEM((9, kw, m), BF16),
                 pltpu.VMEM((9, kw, kd), BF16),
@@ -721,8 +750,8 @@
                 pltpu.VMEM((own, lanes), F32),
                 pltpu.VMEM((own, lanes), BF16),
                 pltpu.VMEM((own, lanes), BF16),
-                pltpu.VMEM((4 * ov, kd), BF16),
-                pltpu.VMEM((4 * ov, kd), BF16),
+                pltpu.VMEM((4 * (mrows + dr), lanes), BF16),
+                pltpu.VMEM((4 * ov, lanes), BF16),
                 pltpu.VMEM((max(4 * ov, 4 * halo), nv), F32),
                 pltpu.VMEM((layer, nv), F32),
                 pltpu.VMEM((layer, nv), F32),
@@ -737,8 +766,8 @@
                 dma((2, 4)),
                 dma((5, 4)),
                 dma((5, 4)),
-                dma((2, 4)),
-                dma((2, 4)),
+                dma((3, 4)),
+                dma((3, 4)),
                 dma((2,)),
                 dma((2,)),
             ],
@@ -757,7 +786,7 @@
             out_shape=[jax.ShapeDtypeStruct((own, nv), F32)] * 2,
             in_specs=[vm, vm],
             out_specs=[anywhere, anywhere],
-            scratch_shapes=[dma((2,))],
+            scratch_shapes=[dma((2 * comps,))],
         )(*[pltpu.with_memory_space_constraint(o, pltpu.VMEM) for o in out])
         return tuple(o.reshape(residual.shape) for o in out)
 

time: 25.6 us -> 25.4 us (level)
  no operation moved by 1% of the time
where the time goes in v5:
time: 25.4 us; the launch traced here: 25.2 us
  Pallas kernels  24.6 us (97%)
  between operations  0.64 us (3%)
    pallas_call x1, Pallas kernels, per_device(): pl.pallas_call(functools.partial(kernel, gx, gy, (comps, cx, cy, nv)), ou...  23.6 us
    pallas_call x1, Pallas kernels, per_device(): pl.pallas_call(emit, out_shape=[jax.ShapeDtypeStruct((own, nv), F32)] * 2...  0.92 us

profile of v5, /device:TPU:0, one launch (start us, length us, event | category | flops | bytes accessed | tf_op | source)
XLA Modules:
  0.0 25.2 jit_solution(3804886948303954733)
XLA Ops:
  0.6 23.6 %shard_map.86 = (f32[768,128]{1,0:T(8,128)S(1)}, f32[768,128]{1,0:T(8,128)S(1)}) custom-call(f32[768,128]{1,0:T(8,128)} %bitcast.9, f32[16,16]{1,0:T(8,128)} %stiff_hbm.1, bf16[1024,1024]{1,0:T(8,128)(2,1)} %bitcast.8, bf16[8,1024]{1,0:T(8,128)(2,1)} %bitcast.10, bf16[8,256]{1,0:T(8,128)(2,1)} %bitcast.11, s32[4,64]{1,0:T(4,128)} %bitcast.12, s32[1,32]{1,0:T(1,128)} %bitcast.13), custom_call_target="tpu_custom_call" | custom-call | tf_op jit(solution)/shard_map/pallas_call | solution.py:701
  24.3 0.9 %shard_map.87 = (f32[768,128]{1,0:T(8,128)}, f32[768,128]{1,0:T(8,128)}) custom-call(f32[768,128]{1,0:T(8,128)S(1)} %get-tuple-element.6.sol_ref, f32[768,128]{1,0:T(8,128)S(1)} %get-tuple-element.7.fin_ref), custom_call_target="tpu_custom_call" | custom-call | tf_op jit(solution)/shard_map/pallas_call | solution.py:784

commit v6 on v5

--- a/solution.py
+++ b/solution.py
@@ -461,13 +461,13 @@
         msg_s[p, ov + 3 * halo :, :] = made_first[4 * dr2 + p * crows : 4 * dr2 + (p + 1) * crows]
         dsend[p, :dr2, :] = made_first[p * dr2 : (p + 1) * dr2]
         dsend[p, dr2:, :] = made_rest[p * (dr - dr2) : (p + 1) * (dr - dr2)]
+    wait_back = trade(
+        lambda p: [remote(msg_s.at[p], ybuf.at[pl.ds(p * mrows, mrows)], nsem_s.at[1, p], nsem_r.at[1, p], up[p])],
+        has_up, has_down,
+    )
     wait_corners = trade(
         lambda p: [remote(dsend.at[p], ybuf.at[pl.ds(ycorner + p * dr, dr)], dsem_s.at[0, p], dsem_r.at[0, p], cdev[p])],
         has_c, has_cd,
-    )
-    wait_back = trade(
-        lambda p: [remote(msg_s.at[p], ybuf.at[pl.ds(p * mrows, mrows)], nsem_s.at[1, p], nsem_r.at[1, p], up[p])],
-        has_up, has_down,
     )
     go(1)
     for h in range(2):

time: 25.4 us -> 25.3 us (level)
  no operation moved by 1% of the time
where the time goes in v6:
time: 25.3 us; the launch traced here: 25.1 us
  Pallas kernels  24.5 us (97%)
  between operations  0.64 us (3%)
    pallas_call x1, Pallas kernels, per_device(): pl.pallas_call(functools.partial(kernel, gx, gy, (comps, cx, cy, nv)), ou...  23.6 us
    pallas_call x1, Pallas kernels, per_device(): pl.pallas_call(emit, out_shape=[jax.ShapeDtypeStruct((own, nv), F32)] * 2...  0.92 us

profile of v6, /device:TPU:0, one launch (start us, length us, event | category | flops | bytes accessed | tf_op | source)
XLA Modules:
  0.0 25.1 jit_solution(5326167360397478722)
XLA Ops:
  0.6 23.6 %shard_map.86 = (f32[768,128]{1,0:T(8,128)S(1)}, f32[768,128]{1,0:T(8,128)S(1)}) custom-call(f32[768,128]{1,0:T(8,128)} %bitcast.9, f32[16,16]{1,0:T(8,128)} %stiff_hbm.1, bf16[1024,1024]{1,0:T(8,128)(2,1)} %bitcast.8, bf16[8,1024]{1,0:T(8,128)(2,1)} %bitcast.10, bf16[8,256]{1,0:T(8,128)(2,1)} %bitcast.11, s32[4,64]{1,0:T(4,128)} %bitcast.12, s32[1,32]{1,0:T(1,128)} %bitcast.13), custom_call_target="tpu_custom_call" | custom-call | tf_op jit(solution)/shard_map/pallas_call | solution.py:701
  24.2 0.9 %shard_map.87 = (f32[768,128]{1,0:T(8,128)}, f32[768,128]{1,0:T(8,128)}) custom-call(f32[768,128]{1,0:T(8,128)S(1)} %get-tuple-element.6.sol_ref, f32[768,128]{1,0:T(8,128)S(1)} %get-tuple-element.7.fin_ref), custom_call_target="tpu_custom_call" | custom-call | tf_op jit(solution)/shard_map/pallas_call | solution.py:784
